TPU v7x, 32 devices: a whole 2x2x4 slice. The times are simulated.
32 devices in a mesh: gx: 4 (over y, x), gy: 8 (over z, core).
Axes of the slice: x: 2, y: 2, z: 4, core: 2. Of those that a mesh axis runs over, the one named last changes fastest.
Arguments:
- features: bfloat16 [4, 8, 512, 128], P('gx', 'gy'), may hold values from -6 to 6
- coords: float32 [4, 8, 3, 512], P('gx', 'gy'), may hold values from 0 to 1
- migrate_x_slots: int32 [4, 8, 2, 32], P('gx', 'gy'), may hold values from 0 to 511, as said below
- migrate_y_slots: int32 [4, 8, 2, 32], P('gx', 'gy'), may hold values from 0 to 511, as said below
- ghost_slots: int32 [4, 8, 256], P('gx', 'gy'), may hold values from 0 to 511, as said below
- neighbours: int32 [4, 8, 512, 16], P('gx', 'gy'), may hold values from 0 to 2815, as said below
- source_weight: bfloat16 [128, 128], replicated, may hold values from -0.5 to 0.5
- target_weight: bfloat16 [128, 128], replicated, may hold values from -0.5 to 0.5
- radial_weight: float32 [8, 128], replicated, may hold values from -2 to 2
- environ_first: bfloat16 [128, 128], replicated, may hold values from -0.5 to 0.5
- mixing_first: bfloat16 [128, 128], replicated, may hold values from -0.5 to 0.5
- coupler_first: bfloat16 [128, 128], replicated, may hold values from -0.5 to 0.5
- environ_second: bfloat16 [128, 128], replicated, may hold values from -0.5 to 0.5
- mixing_second: bfloat16 [128, 128], replicated, may hold values from -0.5 to 0.5
- coupler_second: bfloat16 [128, 128], replicated, may hold values from -0.5 to 0.5
- readout: bfloat16 [128], replicated, may hold values from -0.5 to 0.5
Outputs:
- forces: float32 [4, 8, 3, 512], P('gx', 'gy')
- energies: float32 [4, 8, 512], P('gx', 'gy')
Inputs may be any that keep to these rules, and one draw needn't show every extreme that they name: `migrate_x_slots`: in each device's two rows the 64 slots are distinct. `migrate_y_slots`: in each device's two rows the 64 slots are distinct. `ghost_slots`: each device's 256 slots are distinct. `neighbours`: an entry of atom i is either a slot of the same device other than i, or 512 + s * 256 + g with s in 0..8 but never 4 and g below 256, naming ghost g of the device at grid offset (s // 3 - 1, s % 3 - 1), periodic.
All inputs are finite; a program needn't handle non-finite values.
Results may differ from a plain program's by a relative error of at most 0.005.
Values may be sent and summed in bfloat16 or wider, within the bound.
A program may use at most 64 MiB of HBM per device.

v0:
```python
import functools
import math

import jax
import jax.numpy as jnp
from jax import lax
from jax.experimental import pallas as pl
from jax.experimental.pallas import tpu as pltpu
from jax.sharding import PartitionSpec as P

soften = 0.25
cutoff = 2.0


def split_three(value):
    top = value.astype(jnp.bfloat16).astype(jnp.float32)
    rest = value - top
    middle = rest.astype(jnp.bfloat16).astype(jnp.float32)
    return (top, middle, rest - middle)


def sigmoid(value):
    return 0.5 * jnp.tanh(0.5 * value) + 0.5


def turned(weight):
    return weight.astype(jnp.float32).T.astype(jnp.bfloat16)


def edge_kernel(
    block_atoms,
    index_ref,
    table_ref,
    source_ref,
    place_ref,
    own_ref,
    radial_far,
    environ_first_far,
    mixing_first_far,
    coupler_first_far,
    environ_second_far,
    mixing_second_far,
    coupler_second_far,
    readout_far,
    scatter_ref,
    atom_ref,
    energy_ref,
    radial_ref,
    environ_first,
    mixing_first,
    coupler_first,
    environ_second,
    mixing_second,
    coupler_second,
    readout_ref,
    fetch_sem,
    index_sem,
    index_smem,
    gathered,
    scalars,
    results,
    saved,
    forward_weights,
    backward_weights,
    environ_turned,
    radial_in,
    radial_out,
    pick_weights,
    place_split,
):
    slots_per, atom_count = index_ref.shape
    breadth = table_ref.shape[1]
    groups = place_ref.shape[1]
    f32 = jnp.float32
    bf16 = jnp.bfloat16
    lists = [
        pltpu.make_async_copy(
            index_ref.at[slot],
            index_smem.at[pl.ds(slot * atom_count, atom_count)],
            index_sem.at[slot],
        )
        for slot in range(slots_per)
    ]
    for fetch in lists:
        fetch.start()
    fetches = [
        pltpu.make_async_copy(far, near, fetch_sem.at[n])
        for n, (far, near) in enumerate(
            (
                (radial_far, radial_ref),
                (environ_first_far, environ_first),
                (mixing_first_far, mixing_first),
                (coupler_first_far, coupler_first),
                (environ_second_far, environ_second),
                (mixing_second_far, mixing_second),
                (coupler_second_far, coupler_second),
                (readout_far, readout_ref),
            )
        )
    ]
    for fetch in fetches:
        fetch.start()

    for fetch in lists:
        fetch.wait()
    step = math.gcd(atom_count, 16)

    @pl.loop(0, slots_per)
    def _(slot):
        @pl.loop(0, atom_count // step)
        def _(part):
            base = pl.multiple_of(part * step, step)
            start = slot * atom_count + base
            for u in range(step):
                row = index_smem[start + u]
                gathered[slot, pl.ds(base + u, 1), :] = table_ref[pl.ds(row, 1), :]

    for fetch in fetches:
        fetch.wait()

    forward_weights[0, :, :breadth] = environ_first[...]
    forward_weights[0, :, breadth:] = mixing_first[...]
    forward_weights[1, :, :breadth] = environ_second[...]
    forward_weights[1, :, breadth:] = mixing_second[...]
    backward_weights[0, :, :breadth] = turned(coupler_first[...])
    backward_weights[0, :, breadth:] = turned(mixing_first[...])
    backward_weights[1, :, :breadth] = turned(coupler_second[...])
    backward_weights[1, :, breadth:] = turned(mixing_second[...])
    environ_turned[0] = turned(environ_first[...])
    environ_turned[1] = turned(environ_second[...])
    w_top, w_mid, w_low = split_three(radial_ref[...])
    basis = radial_ref.shape[0]
    lead = jnp.zeros((8, breadth), f32)
    tail = jnp.zeros((breadth - 8 - 6 * basis, breadth), f32)
    radial_in[...] = jnp.concatenate(
        [lead, w_top, w_mid, w_low, w_top, w_mid, w_top, tail], axis=0
    ).astype(bf16)
    wide = jnp.concatenate(
        [lead, w_top, w_mid, jnp.zeros((breadth - 8 - 2 * basis, breadth), f32)], axis=0
    ).T.astype(bf16)
    radial_out[:breadth, :] = wide
    radial_out[breadth:, :] = wide
    lane_id = lax.broadcasted_iota(jnp.int32, (breadth, breadth), 1)
    for k in range(4):
        pick_weights[k * breadth : (k + 1) * breadth, :] = (
            jnp.where(lane_id == k, 1.0, 0.0).astype(bf16)
        )
    places = place_ref[...].reshape(3 * groups, breadth)
    p_top, p_mid, p_low = split_three(places)
    place_split[...] = jnp.concatenate([p_top, p_mid, p_low], axis=0).astype(bf16)

    def chosen(slot):
        index = index_ref[pl.ds(slot, 1), :]
        low = lax.rem(index, breadth)
        high = lax.div(index, breadth)
        rows = lax.broadcasted_iota(jnp.int32, (breadth, atom_count), 0)
        one_hot = jnp.where(rows == low, 1.0, 0.0).astype(bf16)
        group_rows = lax.broadcasted_iota(jnp.int32, (groups, atom_count), 0)
        return (one_hot, group_rows == high)

    @pl.loop(0, slots_per, unroll=4)
    def _(slot):
        one_hot, in_group = chosen(slot)
        found = jnp.dot(place_split[...], one_hot, preferred_element_type=f32)
        size = 3 * groups
        found = found[:size] + found[size : 2 * size] + found[2 * size :]
        offsets = []
        for k in range(3):
            far = jnp.sum(
                jnp.where(in_group, found[k * groups : (k + 1) * groups], 0.0),
                axis=0,
                keepdims=True,
            )
            offsets.append(far - own_ref[k : k + 1, :])
        square = offsets[0] * offsets[0] + offsets[1] * offsets[1] + offsets[2] * offsets[2]
        length = jnp.sqrt(square + soften)
        inverse = 1.0 / length
        scaled = length / cutoff
        smooth = (1.0 - scaled * scaled) ** 2
        angle = scaled * math.pi
        sine = jnp.sin(angle)
        cosine = jnp.cos(angle)
        factor = inverse * smooth
        before, now = (jnp.zeros_like(sine), sine)
        waves = []
        for _ in range(basis):
            waves.append(now * factor)
            before, now = (now, 2.0 * cosine * now - before)
        bessel = jnp.concatenate(waves, axis=0)
        b_top, b_mid, b_low = split_three(bessel)
        blank = jnp.zeros_like(sine)
        head = [offsets[k] * inverse for k in range(3)] + [smooth] + [blank] * 4
        spare = jnp.zeros((breadth - 8 - 6 * basis, atom_count), f32)
        stack = jnp.concatenate(
            head + [b_top, b_top, b_top, b_mid, b_mid, b_low, spare], axis=0
        )
        scalars[slot] = stack.T
        saved[slot] = jnp.concatenate(offsets + [length, sine, cosine, blank, blank], axis=0)

    norm_scale = 1.0 / math.sqrt(slots_per)
    edges = slots_per * block_atoms
    cube = (slots_per, block_atoms, breadth)
    readout_row = readout_ref[...].astype(f32)[None]
    couplers = (coupler_first, coupler_second)
    ee_lane = lax.broadcasted_iota(jnp.int32, (edges, breadth), 1) == 4

    def product(left, right):
        return jnp.dot(left.astype(bf16), right, preferred_element_type=f32)

    @pl.loop(0, atom_count // block_atoms, unroll=1)
    def _(block):
        first = pl.multiple_of(block * block_atoms, block_atoms)
        atoms = pl.ds(first, block_atoms)
        narrow = scalars[:, atoms, :]
        radial = product(narrow.reshape(edges, breadth), radial_in[...]).reshape(cube)
        rows = gathered[:, atoms, :]
        paired = rows + source_ref[atoms, :][None] + radial
        gate = sigmoid(paired)
        value = paired * gate
        slopes = [gate + value * (1.0 - gate)]
        hidden = value.reshape(edges, breadth).astype(bf16)
        direction = [jnp.broadcast_to(narrow[:, :, k : k + 1], cube) for k in range(3)]
        smooth = jnp.broadcast_to(narrow[:, :, 3:4], cube)
        kept = []
        for layer in range(2):
            both = jnp.dot(hidden, forward_weights[layer], preferred_element_type=f32)
            carried = both[:, :breadth].reshape(cube)
            eased = smooth * carried
            environment = [
                jnp.sum(direction[k] * eased, axis=0) * norm_scale for k in range(3)
            ]
            coupled = direction[0] * environment[0][None]
            coupled = coupled + direction[1] * environment[1][None]
            coupled = coupled + direction[2] * environment[2][None]
            mixed = both[:, breadth:] + product(
                coupled.reshape(edges, breadth), couplers[layer][...]
            )
            mixed = mixed.reshape(cube)
            gate = sigmoid(mixed)
            value = mixed * gate
            slopes.append(gate + value * (1.0 - gate))
            kept.append((carried, eased, environment))
            if layer == 0:
                hidden = value.reshape(edges, breadth).astype(bf16)
        edge_energy = jnp.sum(value * readout_row, axis=2, keepdims=True)
        flow = smooth * readout_row
        sums = None
        for layer in (1, 0):
            carried, eased, environment = kept[layer]
            mixed_grad = flow * slopes[layer + 1]
            back = product(mixed_grad.reshape(edges, breadth), backward_weights[layer])
            coupled_grad = back[:, :breadth].reshape(cube)
            environment_grad = [
                jnp.sum(direction[k] * coupled_grad, axis=0) * norm_scale for k in range(3)
            ]
            spread = direction[0] * environment_grad[0][None]
            spread = spread + direction[1] * environment_grad[1][None]
            spread = spread + direction[2] * environment_grad[2][None]
            parts = [
                coupled_grad * environment[k][None] + eased * environment_grad[k][None]
                for k in range(3)
            ] + [carried * spread]
            sums = parts if sums is None else [x + y for x, y in zip(sums, parts)]
            flow = back[:, breadth:].reshape(cube) + product(
                (smooth * spread).reshape(edges, breadth), environ_turned[layer]
            ).reshape(cube)
        paired_grad = (flow * slopes[0]).reshape(edges, breadth)
        high = paired_grad.astype(bf16)
        low = (paired_grad - high.astype(f32)).astype(bf16)
        total = jnp.dot(
            jnp.concatenate([high, low], axis=1), radial_out[...], preferred_element_type=f32
        )
        total = total + jnp.dot(
            jnp.concatenate([x.reshape(edges, breadth).astype(bf16) for x in sums], axis=1),
            pick_weights[...],
            preferred_element_type=f32,
        )
        total = jnp.where(
            ee_lane, jnp.broadcast_to(edge_energy, cube).reshape(edges, breadth), total
        )
        results[:, atoms, :] = total.reshape(cube)

    scatter_ref[...] = jnp.zeros(scatter_ref.shape, f32)
    atom_ref[...] = jnp.zeros(atom_ref.shape, f32)
    energy_ref[...] = jnp.zeros(energy_ref.shape, f32)

    @pl.loop(0, slots_per, unroll=1)
    def _(slot):
        flat = results[slot].T
        data = saved[slot]
        offsets = [data[k : k + 1] for k in range(3)]
        length, sine, cosine = (data[3:4], data[4:5], data[5:6])
        inverse = 1.0 / length
        scaled = length / cutoff
        under = 1.0 - scaled * scaled
        smooth = under * under
        direction = [offsets[k] * inverse for k in range(3)]
        sin_before, sin_now = (jnp.zeros_like(sine), sine)
        cos_before, cos_now = (jnp.ones_like(sine), cosine)
        first_sum = jnp.zeros_like(sine)
        second_sum = jnp.zeros_like(sine)
        for b in range(basis):
            grad = flat[8 + b : 9 + b] + flat[8 + basis + b : 9 + basis + b]
            first_sum = first_sum + grad * sin_now
            second_sum = second_sum + grad * (cos_now * ((b + 1) * math.pi / cutoff))
            sin_before, sin_now = (sin_now, 2.0 * cosine * sin_now - sin_before)
            cos_before, cos_now = (cos_now, 2.0 * cosine * cos_now - cos_before)
        edge_energy = flat[4:5]
        smooth_grad = flat[3:4] + edge_energy + first_sum * inverse
        along = flat[0:1] * direction[0] + flat[1:2] * direction[1] + flat[2:3] * direction[2]
        length_grad = smooth * inverse * (second_sum - first_sum * inverse)
        length_grad = length_grad - smooth_grad * under * (2.0 * scaled / cutoff) * 2.0
        length_grad = length_grad - along * inverse
        one_hot, in_group = chosen(slot)
        pieces = []
        atom_rows = []
        for k in range(3):
            grad = flat[k : k + 1] * inverse + length_grad * direction[k]
            atom_rows.append(-grad)
            pieces.append(jnp.where(in_group, jnp.broadcast_to(grad, in_group.shape), 0.0))
        spread = jnp.concatenate(pieces, axis=0)
        top = spread.astype(bf16)
        low = (spread - top.astype(f32)).astype(bf16)
        for piece in (top, low):
            scatter_ref[...] += lax.dot_general(
                piece, one_hot, (((1,), (1,)), ((), ())), preferred_element_type=f32
            )
        blank = jnp.zeros_like(sine)
        atom_ref[...] += jnp.concatenate(atom_rows + [blank] * 5, axis=0)
        energy_ref[...] += edge_energy * smooth


def others(shape):
    here = (lax.axis_index("gx"), lax.axis_index("gy"))
    steps = [(n // 3 - 1, n % 3 - 1) for n in range(9)]

    def at(dx, dy):
        return (
            lax.rem(here[0] + (dx + shape[0]), shape[0]),
            lax.rem(here[1] + (dy + shape[1]), shape[1]),
        )

    return (at, steps)


def greet(shape):
    at, steps = others(shape)
    barrier = pltpu.get_barrier_semaphore()
    for dx, dy in steps:
        if (dx, dy) != (0, 0):
            pl.semaphore_signal(
                barrier, inc=1, device_id=at(dx, dy), device_id_type=pl.DeviceIdType.MESH
            )
    return barrier


def hot_columns(slots, count):
    rows = lax.broadcasted_iota(jnp.int32, (count, slots.shape[1]), 0)
    return jnp.where(rows == slots, 1.0, 0.0)


def share_kernel(
    shape,
    features_far,
    coords,
    slots_x_far,
    slots_y_far,
    ghosts_far,
    neighbours,
    source_weight_far,
    target_weight_far,
    table_ref,
    source_ref,
    place_ref,
    own_ref,
    index_ref,
    features,
    slots_x,
    slots_y,
    ghosts,
    source_weight,
    target_weight,
    fetch_sem,
    holding,
    leaving,
    arriving,
    ghost_rows,
    ghost_places,
    halo_rows,
    halo_places,
    move_send,
    move_recv,
    rows_send,
    rows_recv,
    places_send,
    places_recv,
):
    f32 = jnp.float32
    bf16 = jnp.bfloat16
    mesh_ids = pl.DeviceIdType.MESH
    count, breadth = features.shape
    sent = slots_x.shape[1]
    slots_per = neighbours.shape[1]
    ghost_count = ghosts.shape[1]
    at, steps = others(shape)
    barrier = greet(shape)
    fetches = [
        pltpu.make_async_copy(far, near, fetch_sem.at[n])
        for n, (far, near) in enumerate(
            (
                (features_far, features),
                (slots_x_far, slots_x),
                (slots_y_far, slots_y),
                (ghosts_far, ghosts),
                (source_weight_far, source_weight),
                (target_weight_far, target_weight),
            )
        )
    ]
    for fetch in fetches:
        fetch.start()

    blank = jnp.zeros((5, count), f32)
    pieces = []
    for piece in split_three(coords[...]):
        pieces += [piece, blank]
    pieces.append(jnp.zeros((breadth - 24, count), f32))
    holding[:, breadth:] = jnp.concatenate(pieces, axis=0).T.astype(bf16)
    for fetch in fetches:
        fetch.wait()
    holding[:, :breadth] = features[...]
    slots_x = jnp.concatenate([slots_x[0:1, :], slots_x[1:2, :]], axis=1)
    slots_y = jnp.concatenate([slots_y[0:1, :], slots_y[1:2, :]], axis=1)
    both = jnp.concatenate([slots_x, slots_y], axis=1)
    picks = hot_columns(both, count).T.astype(bf16)
    ghost_hot = hot_columns(ghosts[...], count)
    ghost_picks = ghost_hot.T.astype(bf16)
    ghost_hot = ghost_hot.astype(bf16)
    listed = neighbours[...].astype(f32)
    listed = jnp.concatenate([listed, jnp.zeros((count, breadth - slots_per), f32)], axis=1)
    index_ref[...] = listed.T[:slots_per].astype(jnp.int32)

    for axis, slots in ((0, slots_x), (1, slots_y)):
        chosen = picks[2 * sent * axis : 2 * sent * (axis + 1)]
        payload = jnp.dot(chosen, holding[...], preferred_element_type=f32).astype(bf16)
        leaving[axis, 0] = payload[:sent]
        leaving[axis, 1] = payload[sent:]
        put = hot_columns(slots, count)
        hit = jnp.max(put, axis=1, keepdims=True) > 0.5
        put = put.astype(bf16)
        if axis == 0:
            pl.semaphore_wait(barrier, 8)
        copies = []
        for way, stride in ((0, 1), (1, -1)):
            copy = pltpu.make_async_remote_copy(
                src_ref=leaving.at[axis, way],
                dst_ref=arriving.at[axis, way],
                send_sem=move_send.at[axis, way],
                recv_sem=move_recv.at[axis, way],
                device_id=at(stride, 0) if axis == 0 else at(0, stride),
                device_id_type=mesh_ids,
            )
            copy.start()
            copies.append(copy)
        for copy in copies:
            copy.wait()
        came = arriving[axis].reshape(2 * sent, 2 * breadth)
        moved = jnp.dot(put, came, preferred_element_type=f32)
        holding[...] = jnp.where(hit, moved, holding[...].astype(f32)).astype(bf16)

    rows = holding[:, :breadth]
    target = jnp.dot(rows, target_weight[...], preferred_element_type=f32).astype(bf16)
    ghost_rows[...] = jnp.dot(ghost_picks, target, preferred_element_type=f32).astype(bf16)
    flat = holding[:, breadth:].astype(f32).T[:24]
    ghost_flat = jnp.dot(flat.astype(bf16), ghost_hot, preferred_element_type=f32)
    ghost_places[...] = ghost_flat[:8] + ghost_flat[8:16] + ghost_flat[16:24]
    copies = {}
    for n, (dx, dy) in enumerate(steps):
        if (dx, dy) == (0, 0):
            continue
        copies[n] = []
        for source, landing, send, recv in (
            (ghost_places, halo_places, places_send, places_recv),
            (ghost_rows, halo_rows, rows_send, rows_recv),
        ):
            copy = pltpu.make_async_remote_copy(
                src_ref=source,
                dst_ref=landing.at[n],
                send_sem=send.at[n],
                recv_sem=recv.at[n],
                device_id=at(-dx, -dy),
                device_id_type=mesh_ids,
            )
            copy.start()
            copies[n].append(copy)
    table_ref[:count, :] = target.astype(f32)
    source_ref[...] = (
        jnp.dot(rows, source_weight[...], preferred_element_type=f32).astype(bf16).astype(f32)
    )
    mine = flat[:8] + flat[8:16] + flat[16:24]
    own_ref[...] = mine
    place_ref[...] = jnp.zeros(place_ref.shape, f32)
    own_groups = count // breadth
    for k in range(3):
        for g in range(own_groups):
            place_ref[k, g : g + 1, :] = mine[k : k + 1, g * breadth : (g + 1) * breadth]
    ghost_groups = ghost_count // breadth
    for n in range(9):
        rows_at = pl.ds(count + n * ghost_count, ghost_count)
        if n not in copies:
            table_ref[rows_at, :] = jnp.zeros((ghost_count, breadth), f32)
            continue
        for copy in copies[n]:
            copy.wait()
        table_ref[rows_at, :] = halo_rows[n].astype(f32)
        places = halo_places[n]
        for k in range(3):
            for g in range(ghost_groups):
                group = own_groups + n * ghost_groups + g
                place_ref[k, group : group + 1, :] = places[
                    k : k + 1, g * breadth : (g + 1) * breadth
                ]


def return_kernel(
    shape, scattered, by_atom, ghosts, force_ref, leaving, arriving, send_sem, recv_sem
):
    f32 = jnp.float32
    bf16 = jnp.bfloat16
    count = by_atom.shape[1]
    breadth = scattered.shape[2]
    ghost_groups = ghosts.shape[1] // breadth
    own_groups = count // breadth
    at, steps = others(shape)
    barrier = greet(shape)
    blank = jnp.zeros((5, breadth), f32)
    for n in range(9):
        for g in range(ghost_groups):
            group = own_groups + n * ghost_groups + g
            piece = [scattered[k, group : group + 1, :] for k in range(3)]
            leaving[n, :, g * breadth : (g + 1) * breadth] = jnp.concatenate(
                piece + [blank], axis=0
            )
    spots = hot_columns(ghosts[...], count).T.astype(bf16)
    pl.semaphore_wait(barrier, 8)
    copies = []
    for n, (dx, dy) in enumerate(steps):
        if (dx, dy) == (0, 0):
            continue
        copy = pltpu.make_async_remote_copy(
            src_ref=leaving.at[n],
            dst_ref=arriving.at[n],
            send_sem=send_sem.at[n],
            recv_sem=recv_sem.at[n],
            device_id=at(dx, dy),
            device_id_type=pl.DeviceIdType.MESH,
        )
        copy.start()
        copies.append((n, copy))
    total = leaving[4]
    for n, copy in copies:
        copy.wait()
        total = total + arriving[n]
    stack = jnp.concatenate(split_three(total), axis=0).astype(bf16)
    back = jnp.dot(stack, spots, preferred_element_type=f32)
    back = back[:8] + back[8:16] + back[16:24]
    for k in range(3):
        own = jnp.concatenate([scattered[k, g : g + 1, :] for g in range(own_groups)], axis=1)
        force_ref[k : k + 1, :] = -(own + by_atom[k : k + 1, :] + back[k : k + 1, :])


def per_device(
    shape,
    features,
    coords,
    migrate_x_slots,
    migrate_y_slots,
    ghost_slots,
    neighbours,
    source_weight,
    target_weight,
    radial_weight,
    environ_first,
    mixing_first,
    coupler_first,
    environ_second,
    mixing_second,
    coupler_second,
    readout,
):
    features = features[0, 0]
    coords = coords[0, 0]
    neighbours = neighbours[0, 0]
    ghosts = ghost_slots.reshape(1, -1)
    count, breadth = features.shape
    slots_per = neighbours.shape[1]
    ghost_count = ghosts.shape[1]
    sent = migrate_x_slots.shape[3]
    total_rows = count + 9 * ghost_count
    groups = -(-(total_rows // breadth) // 8) * 8
    f32 = jnp.float32
    bf16 = jnp.bfloat16
    vmem = pl.BlockSpec(memory_space=pltpu.VMEM)
    hbm = pl.BlockSpec(memory_space=pltpu.HBM)
    dma = pltpu.SemaphoreType.DMA
    table, source_rows, places, own, by_slot = pl.pallas_call(
        functools.partial(share_kernel, shape),
        out_shape=(
            jax.ShapeDtypeStruct((total_rows, breadth), f32),
            jax.ShapeDtypeStruct((count, breadth), f32),
            jax.ShapeDtypeStruct((3, groups, breadth), f32),
            jax.ShapeDtypeStruct((8, count), f32),
            jax.ShapeDtypeStruct((slots_per, count), jnp.int32),
        ),
        in_specs=[hbm, vmem, hbm, hbm, hbm, vmem, hbm, hbm],
        out_specs=(vmem,) * 5,
        scratch_shapes=[
            pltpu.VMEM((count, breadth), bf16),
            pltpu.VMEM((2, sent), jnp.int32),
            pltpu.VMEM((2, sent), jnp.int32),
            pltpu.VMEM((1, ghost_count), jnp.int32),
            pltpu.VMEM((breadth, breadth), bf16),
            pltpu.VMEM((breadth, breadth), bf16),
            dma((6,)),
            pltpu.VMEM((count, 2 * breadth), bf16),
            pltpu.VMEM((2, 2, sent, 2 * breadth), bf16),
            pltpu.VMEM((2, 2, sent, 2 * breadth), bf16),
            pltpu.VMEM((ghost_count, breadth), bf16),
            pltpu.VMEM((8, ghost_count), f32),
            pltpu.VMEM((9, ghost_count, breadth), bf16),
            pltpu.VMEM((9, 8, ghost_count), f32),
            dma((2, 2)),
            dma((2, 2)),
            dma((9,)),
            dma((9,)),
            dma((9,)),
            dma((9,)),
        ],
        compiler_params=pltpu.CompilerParams(collective_id=0, has_side_effects=True, vmem_limit_bytes=67043328
        ),
        name="share",
    )(
        features,
        coords,
        migrate_x_slots[0, 0],
        migrate_y_slots[0, 0],
        ghosts,
        neighbours,
        source_weight,
        target_weight,
    )
    block_atoms = math.gcd(count, 64)
    cube = (slots_per, count, breadth)
    scattered, by_atom, energies = pl.pallas_call(
        functools.partial(edge_kernel, block_atoms),
        out_shape=(
            jax.ShapeDtypeStruct((3 * groups, breadth), f32),
            jax.ShapeDtypeStruct((8, count), f32),
            jax.ShapeDtypeStruct((1, count), f32),
        ),
        in_specs=[vmem] * 5 + [pl.BlockSpec(memory_space=pltpu.HBM)] * 8,
        out_specs=(vmem,) * 3,
        scratch_shapes=[
            pltpu.VMEM(radial_weight.shape, f32),
        ]
        + [pltpu.VMEM((breadth, breadth), bf16)] * 6
        + [
            pltpu.VMEM((1, breadth), bf16),
            dma((8,)),
            dma((slots_per,)),
            pltpu.SMEM((slots_per * count,), jnp.int32),
            pltpu.VMEM(cube, f32),
            pltpu.VMEM(cube, f32),
            pltpu.VMEM(cube, f32),
            pltpu.VMEM((slots_per, 8, count), f32),
            pltpu.VMEM((2, breadth, 2 * breadth), bf16),
            pltpu.VMEM((2, breadth, 2 * breadth), bf16),
            pltpu.VMEM((2, breadth, breadth), bf16),
            pltpu.VMEM((breadth, breadth), bf16),
            pltpu.VMEM((2 * breadth, breadth), bf16),
            pltpu.VMEM((4 * breadth, breadth), bf16),
            pltpu.VMEM((9 * groups, breadth), bf16),
        ],
        compiler_params=pltpu.CompilerParams(vmem_limit_bytes=67043328),
        name="edges",
    )(
        by_slot,
        table,
        source_rows,
        places,
        own,
        radial_weight,
        environ_first,
        mixing_first,
        coupler_first,
        environ_second,
        mixing_second,
        coupler_second,
        readout[None],
    )
    forces = pl.pallas_call(
        functools.partial(return_kernel, shape),
        out_shape=jax.ShapeDtypeStruct((3, count), f32),
        in_specs=[vmem] * 3,
        out_specs=vmem,
        scratch_shapes=[
            pltpu.VMEM((9, 8, ghost_count), f32),
            pltpu.VMEM((9, 8, ghost_count), f32),
            dma((9,)),
            dma((9,)),
        ],
        compiler_params=pltpu.CompilerParams(collective_id=1, has_side_effects=True, vmem_limit_bytes=67043328
        ),
        name="give_back",
    )(scattered.reshape(3, groups, breadth), by_atom, ghosts)
    return (forces[None, None], energies[None])


def solution(mesh):
    in_specs = (
        P("gx", "gy", None, None),
        P("gx", "gy", None, None),
        P("gx", "gy", None, None),
        P("gx", "gy", None, None),
        P("gx", "gy", None),
        P("gx", "gy", None, None),
        P(),
        P(),
        P(),
        P(),
        P(),
        P(),
        P(),
        P(),
        P(),
        P(),
    )
    out_specs = (P("gx", "gy", None, None), P("gx", "gy", None))
    return jax.shard_map(
        functools.partial(per_device, (mesh.shape["gx"], mesh.shape["gy"])),
        mesh=mesh, in_specs=in_specs, out_specs=out_specs, check_vma=False
    )
```

profile of v0, /device:TPU:0, one launch (start us, length us, event | category | flops | bytes accessed | tf_op | source)
XLA Modules:
  0.0 94.8 jit_solution(8046653664273864387)
XLA Ops:
  0.6 1.3 %copy.22 = f32[1,1,3,512]{3,2,1,0:T(4,128)} copy(f32[1,1,3,512]{3,1,2,0:T(1,128)} %param.17) | data formatting | bytes 12288
  1.9 1.6 %copy.18 = s32[1,1,512,16]{3,2,1,0:T(8,128)} copy(s32[1,1,512,16]{2,3,1,0:T(8,128)} %param.21) | data formatting | bytes 65536 | tf_op args[5]
  3.5 25.3 %share.1 = (f32[2816,128]{1,0:T(8,128)}, f32[512,128]{1,0:T(8,128)}, f32[3,24,128]{2,1,0:T(8,128)}, f32[8,512]{1,0:T(8,128)}, s32[16,512]{1,0:T(8,128)}) custom-call(bf16[512,128]{1,0:T(8,128)(2,1)} %bitcast.13, f32[3,512]{1,0:T(4,128)} %bitcast.15, s32[2,32]{1,0:T(2,128)} %bitcast.19, s32[2,32]{1,0:T(2,128)} %bitcast.20, s32[1,256]{1,0:T(1,128)} %bitcast.17, ...), custom_call_target="tpu_custom_call" | custom-call | tf_op jit(solution)/shard_map/share/pallas_call | solution.py:606
  28.8 56.0 %edges.1 = (f32[72,128]{1,0:T(8,128)}, f32[8,512]{1,0:T(8,128)}, f32[1,512]{1,0:T(1,128)}) custom-call(s32[16,512]{1,0:T(8,128)} %get-tuple-element.10.index_ref, f32[2816,128]{1,0:T(8,128)} %get-tuple-element.11.table_ref, f32[512,128]{1,0:T(8,128)} %get-tuple-element.12.source_ref, f32[3,24,128]{2,1,0:T(8,128)} %get-tuple-element.13.place_ref, ...), custom_call_target="tpu_custom_call" | custom-call | tf_op jit(solution)/shard_map/edges/pallas_call | solution.py:654
  84.8 8.7 %give_back.1 = f32[3,512]{1,0:T(4,128)} custom-call(f32[3,24,128]{2,1,0:T(8,128)} %bitcast.14, f32[8,512]{1,0:T(8,128)} %get-tuple-element.16.by_atom, s32[1,256]{1,0:T(1,128)} %bitcast.18), custom_call_target="tpu_custom_call" | custom-call | tf_op jit(solution)/shard_map/give_back/pallas_call | solution.py:701
  93.5 1.3 %copy.19 = f32[1,1,3,512]{3,1,2,0:T(1,128)} copy(f32[1,1,3,512]{3,2,1,0:T(4,128)} %bitcast.16) | data formatting | bytes 12288
where the time goes:
time: 95.2 us; the launch traced here: 94.8 us
  Pallas kernels  90 us (95%)
  local copies, waits for them, and re-layouts  4.17 us (4%)
    pallas_call x1, Pallas kernels, per_device(): pl.pallas_call(functools.partial(edge_kernel, block_atoms), out_shape=(ja...  56 us
    pallas_call x1, Pallas kernels, per_device(): pl.pallas_call(functools.partial(share_kernel, shape), out_shape=(jax.Sha...  25.3 us
    pallas_call x1, Pallas kernels, per_device(): pl.pallas_call(functools.partial(return_kernel, shape), out_shape=jax.Sha...  8.69 us
    unnamed x3, local copies, waits for them, and re-layouts  4.17 us

commit v1 on v0

--- a/solution.py
+++ b/solution.py
@@ -366,14 +366,12 @@
     slots_x_far,
     slots_y_far,
     ghosts_far,
-    neighbours,
     source_weight_far,
     target_weight_far,
     table_ref,
     source_ref,
     place_ref,
     own_ref,
-    index_ref,
     features,
     slots_x,
     slots_y,
@@ -400,7 +398,6 @@
     mesh_ids = pl.DeviceIdType.MESH
     count, breadth = features.shape
     sent = slots_x.shape[1]
-    slots_per = neighbours.shape[1]
     ghost_count = ghosts.shape[1]
     at, steps = others(shape)
     barrier = greet(shape)
@@ -422,7 +419,7 @@
 
     blank = jnp.zeros((5, count), f32)
     pieces = []
-    for piece in split_three(coords[...]):
+    for piece in split_three(coords[...].reshape(3, count)):
         pieces += [piece, blank]
     pieces.append(jnp.zeros((breadth - 24, count), f32))
     holding[:, breadth:] = jnp.concatenate(pieces, axis=0).T.astype(bf16)
@@ -436,9 +433,6 @@
     ghost_hot = hot_columns(ghosts[...], count)
     ghost_picks = ghost_hot.T.astype(bf16)
     ghost_hot = ghost_hot.astype(bf16)
-    listed = neighbours[...].astype(f32)
-    listed = jnp.concatenate([listed, jnp.zeros((count, breadth - slots_per), f32)], axis=1)
-    index_ref[...] = listed.T[:slots_per].astype(jnp.int32)
 
     for axis, slots in ((0, slots_x), (1, slots_y)):
         chosen = picks[2 * sent * axis : 2 * sent * (axis + 1)]
@@ -528,21 +522,20 @@
     f32 = jnp.float32
     bf16 = jnp.bfloat16
     count = by_atom.shape[1]
-    breadth = scattered.shape[2]
+    breadth = scattered.shape[1]
+    groups = scattered.shape[0] // 3
     ghost_groups = ghosts.shape[1] // breadth
     own_groups = count // breadth
     at, steps = others(shape)
-    barrier = greet(shape)
     blank = jnp.zeros((5, breadth), f32)
     for n in range(9):
         for g in range(ghost_groups):
             group = own_groups + n * ghost_groups + g
-            piece = [scattered[k, group : group + 1, :] for k in range(3)]
+            piece = [scattered[pl.ds(k * groups + group, 1), :] for k in range(3)]
             leaving[n, :, g * breadth : (g + 1) * breadth] = jnp.concatenate(
                 piece + [blank], axis=0
             )
     spots = hot_columns(ghosts[...], count).T.astype(bf16)
-    pl.semaphore_wait(barrier, 8)
     copies = []
     for n, (dx, dy) in enumerate(steps):
         if (dx, dy) == (0, 0):
@@ -565,8 +558,79 @@
     back = jnp.dot(stack, spots, preferred_element_type=f32)
     back = back[:8] + back[8:16] + back[16:24]
     for k in range(3):
-        own = jnp.concatenate([scattered[k, g : g + 1, :] for g in range(own_groups)], axis=1)
-        force_ref[k : k + 1, :] = -(own + by_atom[k : k + 1, :] + back[k : k + 1, :])
+        own = jnp.concatenate(
+            [scattered[pl.ds(k * groups + g, 1), :] for g in range(own_groups)], axis=1
+        )
+        force_ref[k] = -(own + by_atom[k : k + 1, :] + back[k : k + 1, :])
+
+
+def whole_kernel(
+    shape,
+    block_atoms,
+    features_far,
+    coords,
+    slots_x_far,
+    slots_y_far,
+    ghosts_far,
+    neighbours,
+    source_weight_far,
+    target_weight_far,
+    radial_far,
+    environ_first_far,
+    mixing_first_far,
+    coupler_first_far,
+    environ_second_far,
+    mixing_second_far,
+    coupler_second_far,
+    readout_far,
+    force_ref,
+    energy_ref,
+    table_ref,
+    source_ref,
+    place_ref,
+    own_ref,
+    scatter_ref,
+    atom_ref,
+    *scratch,
+):
+    share, edge, back = scratch[:20], scratch[20:42], scratch[42:]
+    ghosts = share[3]
+    share_kernel(
+        shape,
+        features_far,
+        coords,
+        slots_x_far,
+        slots_y_far,
+        ghosts_far,
+        source_weight_far,
+        target_weight_far,
+        table_ref,
+        source_ref,
+        place_ref,
+        own_ref,
+        *share,
+    )
+    edge_kernel(
+        block_atoms,
+        neighbours,
+        table_ref,
+        source_ref,
+        place_ref,
+        own_ref,
+        radial_far,
+        environ_first_far,
+        mixing_first_far,
+        coupler_first_far,
+        environ_second_far,
+        mixing_second_far,
+        coupler_second_far,
+        readout_far,
+        scatter_ref,
+        atom_ref,
+        energy_ref,
+        *edge,
+    )
+    return_kernel(shape, scatter_ref, atom_ref, ghosts, force_ref, *back)
 
 
 def per_device(
@@ -589,11 +653,11 @@
     readout,
 ):
     features = features[0, 0]
-    coords = coords[0, 0]
-    neighbours = neighbours[0, 0]
+    count, breadth = features.shape
+    coords = coords.transpose(0, 2, 1, 3).reshape(3, 1, count)
+    neighbours = neighbours[0, 0].T
     ghosts = ghost_slots.reshape(1, -1)
-    count, breadth = features.shape
-    slots_per = neighbours.shape[1]
+    slots_per = neighbours.shape[0]
     ghost_count = ghosts.shape[1]
     sent = migrate_x_slots.shape[3]
     total_rows = count + 9 * ghost_count
@@ -603,18 +667,23 @@
     vmem = pl.BlockSpec(memory_space=pltpu.VMEM)
     hbm = pl.BlockSpec(memory_space=pltpu.HBM)
     dma = pltpu.SemaphoreType.DMA
-    table, source_rows, places, own, by_slot = pl.pallas_call(
-        functools.partial(share_kernel, shape),
+    block_atoms = math.gcd(count, 64)
+    cube = (slots_per, count, breadth)
+    forces, energies = pl.pallas_call(
+        functools.partial(whole_kernel, shape, block_atoms),
         out_shape=(
-            jax.ShapeDtypeStruct((total_rows, breadth), f32),
-            jax.ShapeDtypeStruct((count, breadth), f32),
-            jax.ShapeDtypeStruct((3, groups, breadth), f32),
-            jax.ShapeDtypeStruct((8, count), f32),
-            jax.ShapeDtypeStruct((slots_per, count), jnp.int32),
+            jax.ShapeDtypeStruct((3, 1, count), f32),
+            jax.ShapeDtypeStruct((1, count), f32),
         ),
-        in_specs=[hbm, vmem, hbm, hbm, hbm, vmem, hbm, hbm],
-        out_specs=(vmem,) * 5,
+        in_specs=[hbm, vmem, hbm, hbm, hbm, vmem] + [hbm] * 10,
+        out_specs=(vmem,) * 2,
         scratch_shapes=[
+            pltpu.VMEM((total_rows, breadth), f32),
+            pltpu.VMEM((count, breadth), f32),
+            pltpu.VMEM((3, groups, breadth), f32),
+            pltpu.VMEM((8, count), f32),
+            pltpu.VMEM((3 * groups, breadth), f32),
+            pltpu.VMEM((8, count), f32),
             pltpu.VMEM((count, breadth), bf16),
             pltpu.VMEM((2, sent), jnp.int32),
             pltpu.VMEM((2, sent), jnp.int32),
@@ -635,32 +704,6 @@
             dma((9,)),
             dma((9,)),
             dma((9,)),
-        ],
-        compiler_params=pltpu.CompilerParams(collective_id=0, has_side_effects=True, vmem_limit_bytes=67043328
-        ),
-        name="share",
-    )(
-        features,
-        coords,
-        migrate_x_slots[0, 0],
-        migrate_y_slots[0, 0],
-        ghosts,
-        neighbours,
-        source_weight,
-        target_weight,
-    )
-    block_atoms = math.gcd(count, 64)
-    cube = (slots_per, count, breadth)
-    scattered, by_atom, energies = pl.pallas_call(
-        functools.partial(edge_kernel, block_atoms),
-        out_shape=(
-            jax.ShapeDtypeStruct((3 * groups, breadth), f32),
-            jax.ShapeDtypeStruct((8, count), f32),
-            jax.ShapeDtypeStruct((1, count), f32),
-        ),
-        in_specs=[vmem] * 5 + [pl.BlockSpec(memory_space=pltpu.HBM)] * 8,
-        out_specs=(vmem,) * 3,
-        scratch_shapes=[
             pltpu.VMEM(radial_weight.shape, f32),
         ]
         + [pltpu.VMEM((breadth, breadth), bf16)] * 6
@@ -680,15 +723,24 @@
             pltpu.VMEM((2 * breadth, breadth), bf16),
             pltpu.VMEM((4 * breadth, breadth), bf16),
             pltpu.VMEM((9 * groups, breadth), bf16),
+            pltpu.VMEM((9, 8, ghost_count), f32),
+            pltpu.VMEM((9, 8, ghost_count), f32),
+            dma((9,)),
+            dma((9,)),
         ],
-        compiler_params=pltpu.CompilerParams(vmem_limit_bytes=67043328),
-        name="edges",
+        compiler_params=pltpu.CompilerParams(
+            collective_id=0, has_side_effects=True, vmem_limit_bytes=67043328
+        ),
+        name="allegro",
     )(
-        by_slot,
-        table,
-        source_rows,
-        places,
-        own,
+        features,
+        coords,
+        migrate_x_slots[0, 0],
+        migrate_y_slots[0, 0],
+        ghosts,
+        neighbours,
+        source_weight,
+        target_weight,
         radial_weight,
         environ_first,
         mixing_first,
@@ -698,22 +750,7 @@
         coupler_second,
         readout[None],
     )
-    forces = pl.pallas_call(
-        functools.partial(return_kernel, shape),
-        out_shape=jax.ShapeDtypeStruct((3, count), f32),
-        in_specs=[vmem] * 3,
-        out_specs=vmem,
-        scratch_shapes=[
-            pltpu.VMEM((9, 8, ghost_count), f32),
-            pltpu.VMEM((9, 8, ghost_count), f32),
-            dma((9,)),
-            dma((9,)),
-        ],
-        compiler_params=pltpu.CompilerParams(collective_id=1, has_side_effects=True, vmem_limit_bytes=67043328
-        ),
-        name="give_back",
-    )(scattered.reshape(3, groups, breadth), by_atom, ghosts)
-    return (forces[None, None], energies[None])
+    return (forces.reshape(1, 3, 1, count).transpose(0, 2, 1, 3), energies[None])
 
 
 def solution(mesh):

time: 95.2 us -> 85.6 us (0.90)
  Pallas kernels: 90 us -> 82.8 us
  local copies, waits for them, and re-layouts: 4.17 us -> 1.92 us
    pallas_call x3 -> x1, Pallas kernels: 90 us -> 82.8 us  [per_device(): pl.pallas_call(functools.partial(whole_kernel, shape, block_atoms), out_s...]
    unnamed x3 -> x6, local copies, waits for them, and re-layouts: 4.17 us -> 1.92 us
where the time goes in v1:
time: 85.6 us; the launch traced here: 85.3 us
  Pallas kernels  82.8 us (97%)
  local copies, waits for them, and re-layouts  1.92 us (2%)
    pallas_call x1, Pallas kernels, per_device(): pl.pallas_call(functools.partial(whole_kernel, shape, block_atoms), out_s...  82.8 us
    unnamed x6, local copies, waits for them, and re-layouts  1.92 us

profile of v1, /device:TPU:0, one launch (start us, length us, event | category | flops | bytes accessed | tf_op | source)
XLA Modules:
  0.0 85.3 jit_solution(4181238285577244889)
XLA Ops:
  0.6 82.8 %allegro.1 = (f32[3,1,512]{2,1,0:T(1,128)}, f32[1,512]{1,0:T(1,128)}) custom-call(bf16[512,128]{1,0:T(8,128)(2,1)} %bitcast.13, f32[3,1,512]{2,1,0:T(1,128)} %bitcast.16, s32[2,32]{1,0:T(2,128)} %bitcast.18, s32[2,32]{1,0:T(2,128)} %bitcast.19, s32[1,256]{1,0:T(1,128)} %bitcast.20, s32[16,512]{1,0:T(8,128)} %bitcast.14, bf16[128,128]{1,0:T(8,128)(2,1)} %source_weight_far.1, ...), custom_call_target="tpu_custom_call" | custom-call | tf_op jit(solution)/shard_map/allegro/pallas_call | solution.py:672
  83.4 0.0 copy-start
  83.4 0.7 copy-done
  84.1 0.0 copy-start.1
  84.1 0.6 copy.21
  84.7 0.1 copy-done.1
  84.7 0.6 copy.22
Async XLA Ops:
  83.4 0.7 copy-start
  84.1 0.7 copy-start.1

commit v2 on v0

v2 whole, which is shorter than its diff:
```python
import functools
import math
import types

import jax
import jax.numpy as jnp
from jax import lax
from jax.experimental import pallas as pl
from jax.experimental.pallas import tpu as pltpu
from jax.sharding import PartitionSpec as P

soften = 0.25
cutoff = 2.0
f32 = jnp.float32
bf16 = jnp.bfloat16


def split_two(value):
    top = value.astype(bf16).astype(f32)
    return (top, value - top)


def split_three(value):
    top = value.astype(bf16).astype(f32)
    rest = value - top
    middle = rest.astype(bf16).astype(f32)
    return (top, middle, rest - middle)


def turned(weight):
    return weight.astype(f32).T.astype(bf16)


def product(left, right):
    return jnp.dot(left, right, preferred_element_type=f32)


def product_nt(left, right):
    return lax.dot_general(left, right, (((1,), (1,)), ((), ())), preferred_element_type=f32)


def product_tn(left, right):
    return lax.dot_general(left, right, (((0,), (0,)), ((), ())), preferred_element_type=f32)


def gate_of(half):
    lift = 1.0 + jnp.tanh(half)
    value = half * lift
    return value, lift + value * (2.0 - lift)


def prepare_weights(refs, weights, norm_scale):
    (radial_ref, environ, mixing, coupler, readout_ref) = weights
    breadth = radial_ref.shape[1]
    basis = radial_ref.shape[0]
    w_top, w_low = split_two(radial_ref[...])
    row = readout_ref[...].astype(f32)
    blank = functools.partial(jnp.zeros, dtype=f32)
    left = jnp.concatenate([blank((32, breadth)), w_top, w_low, w_top, blank((8, breadth))], axis=0)
    right = jnp.concatenate(
        [blank((32 + 3 * basis, breadth)), row, row, blank((6, breadth))], axis=0
    )
    refs.first[:, :breadth] = (0.5 * left).astype(bf16)
    refs.first[:, breadth:] = (0.5 * right).astype(bf16)
    last = jnp.concatenate(
        [
            jnp.concatenate([w_top, w_low, blank((16, breadth))], axis=0),
            jnp.concatenate([blank((16, breadth)), row, blank((15, breadth))], axis=0),
        ],
        axis=1,
    )
    refs.last[...] = last.astype(bf16)
    for layer in range(2):
        joined = product(environ[layer][...], coupler[layer][...]) * (0.5 * norm_scale)
        mixed = 0.5 * mixing[layer][...].astype(f32)
        refs.forward[layer, :breadth, :] = mixed.astype(bf16)
        refs.forward[layer, breadth:, :] = joined.astype(bf16)
        refs.backward[layer, :, :breadth] = mixed.T.astype(bf16)
        refs.backward[layer, :, breadth:] = joined.T.astype(bf16)


def prepare_places(refs, place_ref):
    breadth = place_ref.shape[2]
    places = place_ref[...].reshape(-1, breadth)
    refs.split[...] = jnp.concatenate(split_three(places), axis=0).astype(bf16)


def prepare_lists(refs, neighbours):
    slots_per, count = neighbours.shape
    tiles = count // 8
    listed = neighbours[...].astype(f32)
    rows = jnp.concatenate([listed[:, a * tiles : (a + 1) * tiles] for a in range(8)], axis=0)
    refs.listed[...] = rows.T.astype(jnp.int32)


def atom_rows(lanes, slots_per):
    rows = lax.broadcasted_iota(jnp.int32, (16, lanes), 0)
    cols = lax.broadcasted_iota(jnp.int32, (16, lanes), 1)
    return jnp.where(rows == cols // slots_per, 1.0, 0.0)


def chosen(refs, tile, groups, width):
    breadth = refs.listed.shape[1]
    index = jnp.concatenate([refs.listed[pl.ds(tile + u, 1), :] for u in range(width)], axis=1)
    low = index & (breadth - 1)
    high = index >> (breadth.bit_length() - 1)
    rows = lax.broadcasted_iota(jnp.int32, (breadth, width * breadth), 0)
    one_hot = jnp.where(rows == low, 1.0, 0.0).astype(bf16)
    group_rows = lax.broadcasted_iota(jnp.int32, (groups, width * breadth), 0)
    return one_hot, group_rows == high


def geometry(refs, own_ref, basis, slots_per):
    tiles, lanes = refs.listed.shape
    groups = refs.split.shape[0] // 9
    size = 3 * groups
    spread = atom_rows(lanes, slots_per)[:8]
    spread = jnp.concatenate([spread] * 3, axis=0).astype(bf16)
    for k in range(3):
        own = jnp.concatenate(
            [own_ref[k : k + 1, a * tiles : (a + 1) * tiles] for a in range(8)], axis=0
        )
        own = jnp.concatenate(split_three(own), axis=0).astype(bf16)
        refs.dense[3 + k] = product_tn(own, spread)

    @pl.loop(0, tiles // 2, unroll=4)
    def _(pair):
        tile = 2 * pair
        one_hot, in_group = chosen(refs, tile, groups, 2)
        found = product(refs.split[...], one_hot)
        found = found[:size] + found[size : 2 * size] + found[2 * size :]
        for k in range(3):
            far = jnp.sum(
                jnp.where(in_group, found[k * groups : (k + 1) * groups], 0.0),
                axis=0,
                keepdims=True,
            )
            for u in range(2):
                refs.dense[k, pl.ds(tile + u, 1), :] = far[:, u * lanes : (u + 1) * lanes]

    @pl.loop(0, tiles // 8)
    def _(group):
        rows = pl.ds(pl.multiple_of(8 * group, 8), 8)
        offsets = [refs.dense[k, rows, :] - refs.dense[3 + k, rows, :] for k in range(3)]
        square = offsets[0] * offsets[0] + offsets[1] * offsets[1] + offsets[2] * offsets[2]
        length = jnp.sqrt(square + soften)
        inverse = 1.0 / length
        scaled = length / cutoff
        smooth = (1.0 - scaled * scaled) ** 2
        angle = scaled * math.pi
        sine = jnp.sin(angle)
        cosine = jnp.cos(angle)
        factor = inverse * smooth
        for n, value in enumerate(offsets + [length, sine, cosine]):
            refs.dense[n, rows, :] = value
        direction = [offsets[k] * inverse for k in range(3)]
        weighted = [direction[k] * smooth for k in range(3)]
        d_top, d_low = zip(*[split_two(x) for x in direction])
        w_top, w_low = zip(*[split_two(x) for x in weighted])
        before, now = (jnp.zeros_like(sine), sine)
        b_top, b_low = [], []
        for _ in range(basis):
            top, low = split_two(now * factor)
            b_top.append(top)
            b_low.append(low)
            before, now = (now, 2.0 * cosine * now - before)
        s_top, s_low = split_two(smooth)
        blank = jnp.zeros_like(sine)
        left = list(d_top) * 2 + list(d_low) + list(w_top) * 2 + list(w_low) + [blank] * 14
        right = list(w_top) + list(w_low) + list(w_top)
        other = list(d_top) + list(d_low) + list(d_top)
        values = left + b_top + b_top + b_low + [s_top, s_low] + [blank] * 6
        for n, value in enumerate(values):
            start = pl.multiple_of(group * 512 + n * 8, 8)
            refs.narrow[pl.ds(start, 8), :] = value
        for n in range(32):
            start = pl.multiple_of(group * 256 + n * 8, 8)
            refs.pairs[0, pl.ds(start, 8), :] = right[n] if n < 9 else blank
            refs.pairs[1, pl.ds(start, 8), :] = other[n - 9] if 9 <= n < 18 else blank


def spread_tiles(refs):
    tiles = refs.listed.shape[0]

    @pl.loop(0, tiles // 8)
    def _(group):
        for member in range(8):
            tile = group * 8 + member
            whole = refs.narrow[pl.ds(group * 512 + member, 64, stride=8), :].astype(bf16)
            rows = pl.ds(group * 256 + member, 32, stride=8)
            refs.lead[tile] = whole[:32]
            refs.upright[tile] = whole.T
            refs.pair[tile, :, :whole.shape[1]] = refs.pairs[0, rows, :].astype(bf16)
            refs.pair[tile, :, whole.shape[1] :] = refs.pairs[1, rows, :].astype(bf16)


def gather_tile(refs, table_ref, target, at, tile, count, slots_per, rows):
    tiles = count // 8
    for row in rows:
        a, slot = divmod(row, slots_per)
        index = refs.index[slot * count + a * tiles + tile]
        target[pl.ds(at + row, 1), :] = table_ref[pl.ds(index, 1), :]


def sub_block(refs, source_ref, gathered, tile, width, mask, slots_per):
    lanes = gathered.shape[1]
    tiles = source_ref.shape[0] // 8
    size = width * lanes
    upright = [refs.upright[tile + u] for u in range(width)]
    pairs = [refs.pair[tile + u] for u in range(width)]
    stacked = jnp.concatenate(upright, axis=0)
    first = product(stacked, refs.first[...])
    grams = [product(upright[u][:, :32], pairs[u]) for u in range(width)]
    yield
    grams = [(x.astype(bf16) * mask) for x in grams]
    source = jnp.concatenate(
        [
            jnp.broadcast_to(source_ref[pl.ds(a * tiles + tile + u, 1), :], (slots_per, lanes))
            for u in range(width)
            for a in range(8)
        ],
        axis=0,
    )
    half = first[:, :lanes] + source + gathered[...]
    flow = first[:, lanes:]
    value, slope = gate_of(half)
    slopes = [slope]
    hidden = value.astype(bf16)
    kept = [hidden]
    yield
    for layer in range(2):
        around = jnp.concatenate(
            [
                product(grams[u][:, :lanes], hidden[u * lanes : (u + 1) * lanes]).astype(bf16)
                for u in range(width)
            ],
            axis=0,
        )
        yield
        half = product(jnp.concatenate([hidden, around], axis=1), refs.forward[layer])
        yield
        value, slope = gate_of(half)
        hidden = value.astype(bf16)
        slopes.append(slope)
        kept.append(hidden)
        yield
    turns = []
    for layer in (1, 0):
        mixed_grad = (flow * slopes[layer + 1]).astype(bf16)
        back = product(mixed_grad, refs.backward[layer])
        yield
        turn = back[:, lanes:].astype(bf16)
        turns.append(turn)
        flow = back[:, :lanes] + jnp.concatenate(
            [
                product(grams[u][:, lanes:], turn[u * lanes : (u + 1) * lanes])
                for u in range(width)
            ],
            axis=0,
        )
        yield
    paired_grad = (flow * slopes[0]).astype(bf16)
    turns = jnp.concatenate(turns, axis=1)
    inputs = jnp.concatenate([kept[1], kept[0]], axis=1)
    cross = []
    for u in range(width):
        rows = slice(u * lanes, (u + 1) * lanes)
        cross.append(product_nt(turns[rows], inputs[rows]))
    ends = product_nt(refs.last[...], jnp.concatenate([paired_grad, kept[2]], axis=1))
    yield
    cross = [x.astype(bf16) * mask[:, :lanes] for x in cross]
    for u in range(width):
        first_row = pl.multiple_of((tile + u) * 96, 96)
        refs.results[pl.ds(first_row, 32), :] = ends[:, u * lanes : (u + 1) * lanes]
        lead = refs.lead[tile + u]
        refs.results[pl.ds(first_row + 32, 32), :] = product(lead, cross[u])
        refs.results[pl.ds(first_row + 64, 32), :] = product_nt(lead, cross[u])


def main_loop(refs, table_ref, source_ref, slots_per, width, blocks):
    count, lanes = source_ref.shape
    tiles = count // 8
    step = width * blocks
    rows = lax.broadcasted_iota(jnp.int32, (lanes, 2 * lanes), 0) // slots_per
    cols = (lax.broadcasted_iota(jnp.int32, (lanes, 2 * lanes), 1) & (lanes - 1)) // slots_per
    refs.mask[...] = jnp.where(rows == cols, 1.0, 0.0).astype(bf16)

    @pl.loop(0, width * blocks)
    def _(tile):
        for part in range(0, lanes, 16):
            gather_tile(
                refs, table_ref, refs.gathered, tile * lanes, tile, count, slots_per,
                range(part, part + 16),
            )

    @pl.loop(0, tiles // step)
    def _(turn):
        tile = turn * step
        after = jnp.minimum(tile + step, tiles - step)
        mask = refs.mask[...]
        lanes_of = [
            sub_block(
                refs,
                source_ref,
                refs.gathered.at[b * width * lanes : (b + 1) * width * lanes],
                tile + b * width,
                width,
                mask,
                slots_per,
            )
            for b in range(blocks)
        ]
        jobs = []
        for t in range(step):
            for part in range(0, lanes, 32):
                jobs.append((t, range(part, part + 32)))
        live = True
        stage = 0
        while live:
            live = False
            for lane in lanes_of:
                for _ in lane:
                    live = True
                    break
            stage += 1
            if stage >= 2:
                for t, part in jobs[:6]:
                    gather_tile(
                        refs, table_ref, refs.gathered, t * lanes, after + t, count,
                        slots_per, part,
                    )
                jobs = jobs[6:]
        for t, part in jobs:
            gather_tile(
                refs, table_ref, refs.gathered, t * lanes, after + t, count, slots_per, part
            )


def finish(refs, scatter_ref, atom_ref, energy_ref, basis, slots_per):
    tiles, lanes = refs.listed.shape
    groups = scatter_ref.shape[0] // 3
    scatter_ref[...] = jnp.zeros(scatter_ref.shape, f32)

    @pl.loop(0, tiles // 8)
    def _(group):
        rows = pl.ds(pl.multiple_of(8 * group, 8), 8)
        offsets = [refs.dense[k, rows, :] for k in range(3)]
        length, sine, cosine = [refs.dense[3 + k, rows, :] for k in range(3)]
        first = group * (8 * 96)

        def taken(row):
            return refs.results[pl.ds(first + row, 8, stride=96), :]

        inverse = 1.0 / length
        scaled = length / cutoff
        under = 1.0 - scaled * scaled
        smooth = under * under
        direction = [offsets[k] * inverse for k in range(3)]
        sin_before, sin_now = (jnp.zeros_like(sine), sine)
        cos_before, cos_now = (jnp.ones_like(sine), cosine)
        first_sum = jnp.zeros_like(sine)
        second_sum = jnp.zeros_like(sine)
        for b in range(basis):
            grad = taken(b) + taken(basis + b)
            first_sum = first_sum + grad * sin_now
            second_sum = second_sum + grad * (cos_now * ((b + 1) * math.pi / cutoff))
            sin_before, sin_now = (sin_now, 2.0 * cosine * sin_now - sin_before)
            cos_before, cos_now = (cos_now, 2.0 * cosine * cos_now - cos_before)
        edge_energy = taken(16)
        left = [2.0 * (taken(32 + k) + taken(38 + k)) for k in range(3)]
        right = [2.0 * (taken(64 + 9 + k) + taken(64 + 15 + k)) for k in range(3)]
        inner = left[0] * direction[0] + left[1] * direction[1] + left[2] * direction[2]
        turn = [right[k] + smooth * left[k] for k in range(3)]
        smooth_grad = inner + edge_energy + first_sum * inverse
        along = turn[0] * direction[0] + turn[1] * direction[1] + turn[2] * direction[2]
        length_grad = smooth * inverse * (second_sum - first_sum * inverse)
        length_grad = length_grad - smooth_grad * under * (2.0 * scaled / cutoff) * 2.0
        length_grad = length_grad - along * inverse
        for k in range(3):
            refs.dense[k, rows, :] = turn[k] * inverse + length_grad * direction[k]
        refs.dense[3, rows, :] = edge_energy * smooth

    sums = atom_rows(lanes, slots_per).astype(bf16)
    for k in range(4):
        total = jnp.zeros((16, tiles), f32)
        for piece in split_three(refs.dense[k]):
            total = total + product_nt(sums, piece.astype(bf16))
        row = jnp.concatenate([total[a : a + 1] for a in range(8)], axis=1)
        if k == 3:
            energy_ref[...] = row
        else:
            atom_ref[k : k + 1, :] = -row

    @pl.loop(0, tiles // 2, unroll=4)
    def _(pair):
        tile = 2 * pair
        one_hot, in_group = chosen(refs, tile, groups, 2)
        pieces = []
        for k in range(3):
            grad = jnp.concatenate(
                [refs.dense[k, pl.ds(tile + u, 1), :] for u in range(2)], axis=1
            )
            pieces.append(jnp.where(in_group, jnp.broadcast_to(grad, in_group.shape), 0.0))
        spread = jnp.concatenate(pieces, axis=0)
        top = spread.astype(bf16)
        low = (spread - top.astype(f32)).astype(bf16)
        both = product_nt(jnp.concatenate([top, low], axis=0), one_hot)
        scatter_ref[...] += both[: 3 * groups] + both[3 * groups :]


def edge_scratch(count, slots_per, breadth, groups, width, blocks):
    tiles = count // 8
    return dict(
        first=pltpu.VMEM((64, 2 * breadth), bf16),
        last=pltpu.VMEM((32, 2 * breadth), bf16),
        forward=pltpu.VMEM((2, 2 * breadth, breadth), bf16),
        backward=pltpu.VMEM((2, breadth, 2 * breadth), bf16),
        split=pltpu.VMEM((9 * groups, breadth), bf16),
        listed=pltpu.VMEM((tiles, breadth), jnp.int32),
        dense=pltpu.VMEM((6, tiles, breadth), f32),
        narrow=pltpu.VMEM((tiles * 64, breadth), f32),
        pairs=pltpu.VMEM((2, tiles * 32, breadth), f32),
        lead=pltpu.VMEM((tiles, 32, breadth), bf16),
        upright=pltpu.VMEM((tiles, breadth, 64), bf16),
        pair=pltpu.VMEM((tiles, 32, 2 * breadth), bf16),
        gathered=pltpu.VMEM((width * blocks * breadth, breadth), f32),
        results=pltpu.VMEM((tiles * 96, breadth), f32),
        mask=pltpu.VMEM((breadth, 2 * breadth), bf16),
        index=pltpu.SMEM((slots_per * count,), jnp.int32),
    )


def others(shape):
    here = (lax.axis_index("gx"), lax.axis_index("gy"))
    steps = [(n // 3 - 1, n % 3 - 1) for n in range(9)]

    def at(dx, dy):
        return (
            lax.rem(here[0] + (dx + shape[0]), shape[0]),
            lax.rem(here[1] + (dy + shape[1]), shape[1]),
        )

    return (at, steps)


def greet(shape):
    at, steps = others(shape)
    barrier = pltpu.get_barrier_semaphore()
    for dx, dy in steps:
        if (dx, dy) != (0, 0):
            pl.semaphore_signal(
                barrier, inc=1, device_id=at(dx, dy), device_id_type=pl.DeviceIdType.MESH
            )
    return barrier


def send(source, landing, sems, device):
    copy = pltpu.make_async_remote_copy(
        src_ref=source,
        dst_ref=landing,
        send_sem=sems[0],
        recv_sem=sems[1],
        device_id=device,
        device_id_type=pl.DeviceIdType.MESH,
    )
    copy.start()
    return copy


def hot_columns(slots, count):
    rows = lax.broadcasted_iota(jnp.int32, (count, slots.shape[1]), 0)
    return jnp.where(rows == slots, 1.0, 0.0)


def fetch_all(pairs, sems):
    copies = [
        pltpu.make_async_copy(far, near, sems.at[n]) for n, (far, near) in enumerate(pairs)
    ]
    for copy in copies:
        copy.start()
    return copies


def whole_kernel(shape, plan, names, *operands):
    r = types.SimpleNamespace(**dict(zip(names, operands)))
    width, blocks = plan
    slots_per, count = r.neighbours.shape
    breadth = r.features.shape[1]
    sent = r.slots_x.shape[1]
    ghost_count = r.ghosts.shape[1]
    basis = r.radial.shape[0]
    own_groups = count // breadth
    ghost_groups = ghost_count // breadth
    at, steps = others(shape)
    around = [n for n, step in enumerate(steps) if step != (0, 0)]
    barrier = greet(shape)
    fetches = fetch_all(
        [
            (r.features_far, r.features),
            (r.slots_x_far, r.slots_x),
            (r.slots_y_far, r.slots_y),
            (r.ghosts_far, r.ghosts),
            (r.source_weight_far, r.source_weight),
            (r.target_weight_far, r.target_weight),
        ],
        r.fetch_sem,
    )
    lists = fetch_all(
        [
            (r.neighbours.at[slot], r.index.at[pl.ds(slot * count, count)])
            for slot in range(slots_per)
        ],
        r.index_sem,
    )
    later = fetch_all(
        [
            (r.radial_far, r.radial),
            (r.readout_far, r.readout),
            (r.environ_first_far, r.environ_first),
            (r.mixing_first_far, r.mixing_first),
            (r.coupler_first_far, r.coupler_first),
            (r.environ_second_far, r.environ_second),
            (r.mixing_second_far, r.mixing_second),
            (r.coupler_second_far, r.coupler_second),
        ],
        r.later_sem,
    )

    holding = r.holding
    blank = jnp.zeros((5, count), f32)
    pieces = []
    for piece in split_three(r.coords[...].reshape(3, count)):
        pieces += [piece, blank]
    pieces.append(jnp.zeros((breadth - 24, count), f32))
    holding[:, breadth:] = jnp.concatenate(pieces, axis=0).T.astype(bf16)
    for fetch in fetches:
        fetch.wait()
    holding[:, :breadth] = r.features[...]
    moves = [
        jnp.concatenate([n[0:1, :], n[1:2, :]], axis=1) for n in (r.slots_x, r.slots_y)
    ]
    picks = hot_columns(jnp.concatenate(moves, axis=1), count).T.astype(bf16)

    def leave(axis):
        chosen_rows = picks[2 * sent * axis : 2 * sent * (axis + 1)]
        payload = product(chosen_rows, holding[...]).astype(bf16)
        r.leaving[axis, 0] = payload[:sent]
        r.leaving[axis, 1] = payload[sent:]
        if axis == 0:
            pl.semaphore_wait(barrier, 8)
        return [
            send(
                r.leaving.at[axis, way],
                r.arriving.at[axis, way],
                (r.move_send.at[axis, way], r.move_recv.at[axis, way]),
                at(stride, 0) if axis == 0 else at(0, stride),
            )
            for way, stride in ((0, 1), (1, -1))
        ]

    def settle(axis, copies):
        put = hot_columns(moves[axis], count)
        hit = jnp.max(put, axis=1, keepdims=True) > 0.5
        for copy in copies:
            copy.wait()
        came = r.arriving[axis].reshape(2 * sent, 2 * breadth)
        moved = product(put.astype(bf16), came)
        holding[...] = jnp.where(hit, moved, holding[...].astype(f32)).astype(bf16)

    copies = leave(0)
    for fetch in later:
        fetch.wait()
    prepare_weights(
        r,
        (
            r.radial,
            (r.environ_first, r.environ_second),
            (r.mixing_first, r.mixing_second),
            (r.coupler_first, r.coupler_second),
            r.readout,
        ),
        1.0 / math.sqrt(slots_per),
    )
    settle(0, copies)
    copies = leave(1)
    prepare_lists(r, r.neighbours)
    ghost_hot = hot_columns(r.ghosts[...], count)
    ghost_picks = ghost_hot.T.astype(bf16)
    ghost_hot = ghost_hot.astype(bf16)
    settle(1, copies)

    flat = holding[:, breadth:].astype(f32).T[:24]
    ghost_flat = product(flat.astype(bf16), ghost_hot)
    ghost_places = ghost_flat[:8] + ghost_flat[8:16] + ghost_flat[16:24]
    r.ghost_places[...] = ghost_places[:4]
    waits = {}
    for n in around:
        dx, dy = steps[n]
        waits[n] = [
            send(
                r.ghost_places,
                r.halo_places.at[n],
                (r.places_send.at[n], r.places_recv.at[n]),
                at(-dx, -dy),
            )
        ]
    rows = holding[:, :breadth]
    half_target = (0.5 * r.target_weight[...].astype(f32)).astype(bf16)
    half_source = (0.5 * r.source_weight[...].astype(f32)).astype(bf16)
    target = product(rows, half_target).astype(bf16)
    r.ghost_rows[...] = product(ghost_picks, target).astype(bf16)

    def send_rows(source, n, device):
        return send(
            source, r.halo_rows.at[n], (r.rows_send.at[n], r.rows_recv.at[n]), device
        )

    cross = {}
    for n in (1, 7):
        cross[n] = send_rows(r.ghost_rows, n, at(-steps[n][0], 0))
    for n in (3, 5):
        waits[n].append(send_rows(r.ghost_rows, n, at(0, -steps[n][1])))

    r.table[:count, :] = target.astype(f32)
    r.source[...] = product(rows, half_source).astype(bf16).astype(f32)
    mine = flat[:8] + flat[8:16] + flat[16:24]
    r.own[...] = mine
    place = r.place
    place[...] = jnp.zeros(place.shape, f32)
    for k in range(3):
        for g in range(own_groups):
            place[k, g : g + 1, :] = mine[k : k + 1, g * breadth : (g + 1) * breadth]
    rows_at = pl.ds(count + 4 * ghost_count, ghost_count)
    r.table[rows_at, :] = jnp.zeros((ghost_count, breadth), f32)

    r.give[...] = jnp.zeros(r.give.shape, f32)
    for n in (1, 7):
        cross[n].wait()
        for dy in (-1, 1):
            waits[n + dy].append(send_rows(r.halo_rows.at[n], n + dy, at(0, -dy)))
    for n in around:
        waits[n][0].wait()
        places = r.halo_places[n]
        for k in range(3):
            for g in range(ghost_groups):
                group = own_groups + n * ghost_groups + g
                place[k, group : group + 1, :] = places[
                    k : k + 1, g * breadth : (g + 1) * breadth
                ]
    prepare_places(r, place)
    geometry(r, r.own, basis, slots_per)
    spread_tiles(r)
    for copy in lists:
        copy.wait()
    for n in around:
        for copy in waits[n][1:]:
            copy.wait()
        rows_at = pl.ds(count + n * ghost_count, ghost_count)
        r.table[rows_at, :] = r.halo_rows[n].astype(f32)

    main_loop(r, r.table, r.source, slots_per, width, blocks)
    finish(r, r.scatter, r.by_atom, r.energy, basis, slots_per)

    scatter = r.scatter
    groups = scatter.shape[0] // 3
    for n in range(9):
        for g in range(ghost_groups):
            group = own_groups + n * ghost_groups + g
            for k in range(3):
                r.give[n, k : k + 1, g * breadth : (g + 1) * breadth] = scatter[
                    pl.ds(k * groups + group, 1), :
                ]
    copies = {}
    for n in around:
        copies[n] = send(
            r.give.at[n], r.got.at[n], (r.give_send.at[n], r.give_recv.at[n]),
            at(*steps[n]),
        )
    spots = hot_columns(r.ghosts[...], count).T.astype(bf16)
    owns = []
    for k in range(3):
        own = jnp.concatenate(
            [scatter[pl.ds(k * groups + g, 1), :] for g in range(own_groups)], axis=1
        )
        owns.append(own + r.by_atom[k : k + 1, :])
    total = r.give[4][:3]
    for n in around:
        copies[n].wait()
        total = total + r.got[n][:3]
    stack = jnp.concatenate(
        [jnp.concatenate([x, jnp.zeros((5, ghost_count), f32)], axis=0) for x in split_three(total)],
        axis=0,
    ).astype(bf16)
    back = product(stack, spots)
    back = back[:8] + back[8:16] + back[16:24]
    for k in range(3):
        r.force[k] = -(owns[k] + back[k : k + 1, :])


def per_device(
    shape,
    features,
    coords,
    migrate_x_slots,
    migrate_y_slots,
    ghost_slots,
    neighbours,
    source_weight,
    target_weight,
    radial_weight,
    environ_first,
    mixing_first,
    coupler_first,
    environ_second,
    mixing_second,
    coupler_second,
    readout,
):
    features = features[0, 0]
    count, breadth = features.shape
    coords = coords.transpose(0, 2, 1, 3).reshape(3, 1, count)
    neighbours = neighbours[0, 0].T
    ghosts = ghost_slots.reshape(1, -1)
    slots_per = neighbours.shape[0]
    ghost_count = ghosts.shape[1]
    sent = migrate_x_slots.shape[3]
    total_rows = count + 9 * ghost_count
    groups = -(-(total_rows // breadth) // 8) * 8
    width, blocks = 4, 4
    vmem = pl.BlockSpec(memory_space=pltpu.VMEM)
    hbm = pl.BlockSpec(memory_space=pltpu.HBM)
    dma = pltpu.SemaphoreType.DMA
    square = pltpu.VMEM((breadth, breadth), bf16)
    inputs = dict(
        features_far=features,
        coords=coords,
        slots_x_far=migrate_x_slots[0, 0],
        slots_y_far=migrate_y_slots[0, 0],
        ghosts_far=ghosts,
        neighbours=neighbours,
        source_weight_far=source_weight,
        target_weight_far=target_weight,
        radial_far=radial_weight,
        environ_first_far=environ_first,
        mixing_first_far=mixing_first,
        coupler_first_far=coupler_first,
        environ_second_far=environ_second,
        mixing_second_far=mixing_second,
        coupler_second_far=coupler_second,
        readout_far=readout[None],
    )
    scratch = dict(
        features=pltpu.VMEM((count, breadth), bf16),
        slots_x=pltpu.VMEM((2, sent), jnp.int32),
        slots_y=pltpu.VMEM((2, sent), jnp.int32),
        ghosts=pltpu.VMEM((1, ghost_count), jnp.int32),
        source_weight=square,
        target_weight=square,
        radial=pltpu.VMEM(radial_weight.shape, f32),
        readout=pltpu.VMEM((1, breadth), bf16),
        environ_first=square,
        mixing_first=square,
        coupler_first=square,
        environ_second=square,
        mixing_second=square,
        coupler_second=square,
        fetch_sem=dma((6,)),
        index_sem=dma((slots_per,)),
        later_sem=dma((8,)),
        table=pltpu.VMEM((total_rows, breadth), f32),
        source=pltpu.VMEM((count, breadth), f32),
        place=pltpu.VMEM((3, groups, breadth), f32),
        own=pltpu.VMEM((8, count), f32),
        scatter=pltpu.VMEM((3 * groups, breadth), f32),
        by_atom=pltpu.VMEM((8, count), f32),
        holding=pltpu.VMEM((count, 2 * breadth), bf16),
        leaving=pltpu.VMEM((2, 2, sent, 2 * breadth), bf16),
        arriving=pltpu.VMEM((2, 2, sent, 2 * breadth), bf16),
        ghost_rows=pltpu.VMEM((ghost_count, breadth), bf16),
        ghost_places=pltpu.VMEM((4, ghost_count), f32),
        halo_rows=pltpu.VMEM((9, ghost_count, breadth), bf16),
        halo_places=pltpu.VMEM((9, 4, ghost_count), f32),
        give=pltpu.VMEM((9, 4, ghost_count), f32),
        got=pltpu.VMEM((9, 4, ghost_count), f32),
        move_send=dma((2, 2)),
        move_recv=dma((2, 2)),
        rows_send=dma((9,)),
        rows_recv=dma((9,)),
        places_send=dma((9,)),
        places_recv=dma((9,)),
        give_send=dma((9,)),
        give_recv=dma((9,)),
        **edge_scratch(count, slots_per, breadth, groups, width, blocks),
    )
    names = tuple(inputs) + ("force", "energy") + tuple(scratch)
    forces, energies = pl.pallas_call(
        functools.partial(whole_kernel, shape, (width, blocks), names),
        out_shape=(
            jax.ShapeDtypeStruct((3, 1, count), f32),
            jax.ShapeDtypeStruct((1, count), f32),
        ),
        in_specs=[vmem if n in ("coords", "neighbours") else hbm for n in inputs],
        out_specs=(vmem,) * 2,
        scratch_shapes=list(scratch.values()),
        compiler_params=pltpu.CompilerParams(
            collective_id=0, has_side_effects=True, vmem_limit_bytes=67043328
        ),
        name="allegro",
    )(*inputs.values())
    return (forces.reshape(1, 3, 1, count).transpose(0, 2, 1, 3), energies[None])


def solution(mesh):
    in_specs = (
        P("gx", "gy", None, None),
        P("gx", "gy", None, None),
        P("gx", "gy", None, None),
        P("gx", "gy", None, None),
        P("gx", "gy", None),
        P("gx", "gy", None, None),
        P(),
        P(),
        P(),
        P(),
        P(),
        P(),
        P(),
        P(),
        P(),
        P(),
    )
    out_specs = (P("gx", "gy", None, None), P("gx", "gy", None))
    return jax.shard_map(
        functools.partial(per_device, (mesh.shape["gx"], mesh.shape["gy"])),
        mesh=mesh, in_specs=in_specs, out_specs=out_specs, check_vma=False
    )
```

time: 95.2 us -> 52.8 us (0.55)
  Pallas kernels: 90 us -> 50 us
  local copies, waits for them, and re-layouts: 4.17 us -> 1.92 us
    pallas_call x3 -> x1, Pallas kernels: 90 us -> 50 us  [per_device(): pl.pallas_call(functools.partial(whole_kernel, shape, (width, blocks), na...]
    unnamed x3 -> x6, local copies, waits for them, and re-layouts: 4.17 us -> 1.92 us
where the time goes in v2:
time: 52.8 us; the launch traced here: 52.6 us
  Pallas kernels  50 us (95%)
  local copies, waits for them, and re-layouts  1.92 us (4%)
  between operations  0.65 us (1%)
    pallas_call x1, Pallas kernels, per_device(): pl.pallas_call(functools.partial(whole_kernel, shape, (width, blocks), na...  50 us
    unnamed x6, local copies, waits for them, and re-layouts  1.92 us

profile of v2, /device:TPU:0, one launch (start us, length us, event | category | flops | bytes accessed | tf_op | source)
XLA Modules:
  0.0 52.6 jit_solution(2095494391528563639)
XLA Ops:
  0.6 50.0 %allegro.1 = (f32[3,1,512]{2,1,0:T(1,128)}, f32[1,512]{1,0:T(1,128)}) custom-call(bf16[512,128]{1,0:T(8,128)(2,1)} %bitcast.13, f32[3,1,512]{2,1,0:T(1,128)} %bitcast.16, s32[2,32]{1,0:T(2,128)} %bitcast.18, s32[2,32]{1,0:T(2,128)} %bitcast.19, s32[1,256]{1,0:T(1,128)} %bitcast.20, s32[16,512]{1,0:T(8,128)} %bitcast.14, bf16[128,128]{1,0:T(8,128)(2,1)} %operands_6_.1, ...), custom_call_target="tpu_custom_call" | custom-call | tf_op jit(solution)/shard_map/allegro/pallas_call | solution.py:796
  50.6 0.0 copy-start
  50.7 0.7 %copy-done = f32[3,1,512]{2,1,0:T(1,128)S(1)} copy-done((f32[3,1,512]{2,1,0:T(1,128)S(1)}, f32[3,1,512]{2,1,0:T(1,128)}, u32[]{:S(2)}) %copy-start) | copy-done | bytes 6168
  51.3 0.0 copy-start.1
  51.3 0.6 %copy.21 = f32[1,1,3,512]{3,1,2,0:T(1,128)} copy(f32[1,1,3,512]{3,1,2,0:T(1,128)S(1)} %bitcast.15) | data formatting | bytes 12288
  51.9 0.1 copy-done.1
  52.0 0.6 %copy.22 = f32[1,1,512]{2,1,0:T(1,128)} copy(f32[1,1,512]{2,1,0:T(1,128)S(1)} %bitcast.17) | data formatting | bytes 4096
Async XLA Ops:
  50.6 0.7 %copy-start = (f32[3,1,512]{2,1,0:T(1,128)S(1)}, f32[3,1,512]{2,1,0:T(1,128)}, u32[]{:S(2)}) copy-start(f32[3,1,512]{2,1,0:T(1,128)} %get-tuple-element.4) | copy-start | bytes 18436
  51.3 0.7 %copy-start.1 = (f32[1,512]{1,0:T(1,128)S(1)}, f32[1,512]{1,0:T(1,128)}, u32[]{:S(2)}) copy-start(f32[1,512]{1,0:T(1,128)} %get-tuple-element.5) | copy-start | bytes 6148

commit v3 on v2

--- a/solution.py
+++ b/solution.py
@@ -82,7 +82,7 @@
 def prepare_places(refs, place_ref):
     breadth = place_ref.shape[2]
     places = place_ref[...].reshape(-1, breadth)
-    refs.split[...] = jnp.concatenate(split_three(places), axis=0).astype(bf16)
+    refs.split[...] = jnp.concatenate(split_two(places), axis=0).astype(bf16)
 
 
 def prepare_lists(refs, neighbours):
@@ -99,20 +99,26 @@
     return jnp.where(rows == cols // slots_per, 1.0, 0.0)
 
 
-def chosen(refs, tile, groups, width):
+def index_of(refs, tile, width):
+    return jnp.concatenate([refs.listed[pl.ds(tile + u, 1), :] for u in range(width)], axis=1)
+
+
+def group_of(refs, tile, groups, width):
     breadth = refs.listed.shape[1]
-    index = jnp.concatenate([refs.listed[pl.ds(tile + u, 1), :] for u in range(width)], axis=1)
-    low = index & (breadth - 1)
-    high = index >> (breadth.bit_length() - 1)
+    high = index_of(refs, tile, width) >> (breadth.bit_length() - 1)
+    return lax.broadcasted_iota(jnp.int32, (groups, width * breadth), 0) == high
+
+
+def hot_of(refs, tile, width):
+    breadth = refs.listed.shape[1]
+    low = index_of(refs, tile, width) & (breadth - 1)
     rows = lax.broadcasted_iota(jnp.int32, (breadth, width * breadth), 0)
-    one_hot = jnp.where(rows == low, 1.0, 0.0).astype(bf16)
-    group_rows = lax.broadcasted_iota(jnp.int32, (groups, width * breadth), 0)
-    return one_hot, group_rows == high
+    return jnp.where(rows == low, 1.0, 0.0).astype(bf16)
 
 
 def geometry(refs, own_ref, basis, slots_per):
     tiles, lanes = refs.listed.shape
-    groups = refs.split.shape[0] // 9
+    groups = refs.split.shape[0] // 6
     size = 3 * groups
     spread = atom_rows(lanes, slots_per)[:8]
     spread = jnp.concatenate([spread] * 3, axis=0).astype(bf16)
@@ -126,9 +132,11 @@
     @pl.loop(0, tiles // 2, unroll=4)
     def _(pair):
         tile = 2 * pair
-        one_hot, in_group = chosen(refs, tile, groups, 2)
+        one_hot = hot_of(refs, tile, 2)
+        in_group = group_of(refs, tile, groups, 2)
+        refs.hot[pair] = one_hot
         found = product(refs.split[...], one_hot)
-        found = found[:size] + found[size : 2 * size] + found[2 * size :]
+        found = found[:size] + found[size:]
         for k in range(3):
             far = jnp.sum(
                 jnp.where(in_group, found[k * groups : (k + 1) * groups], 0.0),
@@ -182,7 +190,7 @@
 def spread_tiles(refs):
     tiles = refs.listed.shape[0]
 
-    @pl.loop(0, tiles // 8)
+    @pl.loop(0, tiles // 8, unroll=2)
     def _(group):
         for member in range(8):
             tile = group * 8 + member
@@ -285,13 +293,10 @@
     cols = (lax.broadcasted_iota(jnp.int32, (lanes, 2 * lanes), 1) & (lanes - 1)) // slots_per
     refs.mask[...] = jnp.where(rows == cols, 1.0, 0.0).astype(bf16)
 
-    @pl.loop(0, width * blocks)
-    def _(tile):
-        for part in range(0, lanes, 16):
-            gather_tile(
-                refs, table_ref, refs.gathered, tile * lanes, tile, count, slots_per,
-                range(part, part + 16),
-            )
+    for tile in range(step):
+        gather_tile(
+            refs, table_ref, refs.gathered, tile * lanes, tile, count, slots_per, range(lanes)
+        )
 
     @pl.loop(0, tiles // step)
     def _(turn):
@@ -336,7 +341,7 @@
             )
 
 
-def finish(refs, scatter_ref, atom_ref, energy_ref, basis, slots_per):
+def finish(refs, scatter_ref, basis):
     tiles, lanes = refs.listed.shape
     groups = scatter_ref.shape[0] // 3
     scatter_ref[...] = jnp.zeros(scatter_ref.shape, f32)
@@ -380,6 +385,22 @@
             refs.dense[k, rows, :] = turn[k] * inverse + length_grad * direction[k]
         refs.dense[3, rows, :] = edge_energy * smooth
 
+    @pl.loop(0, tiles // 2, unroll=4)
+    def _(pair):
+        tile = 2 * pair
+        in_group = group_of(refs, tile, groups, 2)
+        pieces = []
+        for k in range(3):
+            grad = jnp.concatenate(
+                [refs.dense[k, pl.ds(tile + u, 1), :] for u in range(2)], axis=1
+            )
+            pieces.append(jnp.where(in_group, jnp.broadcast_to(grad, in_group.shape), 0.0))
+        spread = jnp.concatenate(pieces, axis=0)
+        scatter_ref[...] += product_nt(spread.astype(bf16), refs.hot[pair])
+
+
+def gather_atoms(refs, atom_ref, energy_ref, slots_per):
+    tiles, lanes = refs.listed.shape
     sums = atom_rows(lanes, slots_per).astype(bf16)
     for k in range(4):
         total = jnp.zeros((16, tiles), f32)
@@ -391,22 +412,6 @@
         else:
             atom_ref[k : k + 1, :] = -row
 
-    @pl.loop(0, tiles // 2, unroll=4)
-    def _(pair):
-        tile = 2 * pair
-        one_hot, in_group = chosen(refs, tile, groups, 2)
-        pieces = []
-        for k in range(3):
-            grad = jnp.concatenate(
-                [refs.dense[k, pl.ds(tile + u, 1), :] for u in range(2)], axis=1
-            )
-            pieces.append(jnp.where(in_group, jnp.broadcast_to(grad, in_group.shape), 0.0))
-        spread = jnp.concatenate(pieces, axis=0)
-        top = spread.astype(bf16)
-        low = (spread - top.astype(f32)).astype(bf16)
-        both = product_nt(jnp.concatenate([top, low], axis=0), one_hot)
-        scatter_ref[...] += both[: 3 * groups] + both[3 * groups :]
-
 
 def edge_scratch(count, slots_per, breadth, groups, width, blocks):
     tiles = count // 8
@@ -415,7 +420,7 @@
         last=pltpu.VMEM((32, 2 * breadth), bf16),
         forward=pltpu.VMEM((2, 2 * breadth, breadth), bf16),
         backward=pltpu.VMEM((2, breadth, 2 * breadth), bf16),
-        split=pltpu.VMEM((9 * groups, breadth), bf16),
+        split=pltpu.VMEM((6 * groups, breadth), bf16),
         listed=pltpu.VMEM((tiles, breadth), jnp.int32),
         dense=pltpu.VMEM((6, tiles, breadth), f32),
         narrow=pltpu.VMEM((tiles * 64, breadth), f32),
@@ -425,6 +430,7 @@
         pair=pltpu.VMEM((tiles, 32, 2 * breadth), bf16),
         gathered=pltpu.VMEM((width * blocks * breadth, breadth), f32),
         results=pltpu.VMEM((tiles * 96, breadth), f32),
+        hot=pltpu.VMEM((tiles // 2, breadth, 2 * breadth), bf16),
         mask=pltpu.VMEM((breadth, 2 * breadth), bf16),
         index=pltpu.SMEM((slots_per * count,), jnp.int32),
     )
@@ -608,18 +614,25 @@
     half_target = (0.5 * r.target_weight[...].astype(f32)).astype(bf16)
     half_source = (0.5 * r.source_weight[...].astype(f32)).astype(bf16)
     target = product(rows, half_target).astype(bf16)
-    r.ghost_rows[...] = product(ghost_picks, target).astype(bf16)
-
-    def send_rows(source, n, device):
+    chunks = [pl.ds(c * (ghost_count // 2), ghost_count // 2) for c in range(2)]
+
+    def send_rows(source, n, c, device):
         return send(
-            source, r.halo_rows.at[n], (r.rows_send.at[n], r.rows_recv.at[n]), device
+            source.at[chunks[c]],
+            r.halo_rows.at[n, chunks[c]],
+            (r.rows_send.at[n, c], r.rows_recv.at[n, c]),
+            device,
         )
 
     cross = {}
-    for n in (1, 7):
-        cross[n] = send_rows(r.ghost_rows, n, at(-steps[n][0], 0))
-    for n in (3, 5):
-        waits[n].append(send_rows(r.ghost_rows, n, at(0, -steps[n][1])))
+    for c in range(2):
+        part = slice(c * (ghost_count // 2), (c + 1) * (ghost_count // 2))
+        r.ghost_rows[part] = product(ghost_picks[part], target).astype(bf16)
+        for n in (1, 7):
+            cross[n, c] = send_rows(r.ghost_rows, n, c, at(-steps[n][0], 0))
+    for c in range(2):
+        for n in (3, 5):
+            waits[n].append(send_rows(r.ghost_rows, n, c, at(0, -steps[n][1])))
 
     r.table[:count, :] = target.astype(f32)
     r.source[...] = product(rows, half_source).astype(bf16).astype(f32)
@@ -634,10 +647,11 @@
     r.table[rows_at, :] = jnp.zeros((ghost_count, breadth), f32)
 
     r.give[...] = jnp.zeros(r.give.shape, f32)
-    for n in (1, 7):
-        cross[n].wait()
-        for dy in (-1, 1):
-            waits[n + dy].append(send_rows(r.halo_rows.at[n], n + dy, at(0, -dy)))
+    for c in range(2):
+        for n in (1, 7):
+            cross[n, c].wait()
+            for dy in (-1, 1):
+                waits[n + dy].append(send_rows(r.halo_rows.at[n], n + dy, c, at(0, -dy)))
     for n in around:
         waits[n][0].wait()
         places = r.halo_places[n]
@@ -659,7 +673,7 @@
         r.table[rows_at, :] = r.halo_rows[n].astype(f32)
 
     main_loop(r, r.table, r.source, slots_per, width, blocks)
-    finish(r, r.scatter, r.by_atom, r.energy, basis, slots_per)
+    finish(r, r.scatter, basis)
 
     scatter = r.scatter
     groups = scatter.shape[0] // 3
@@ -676,6 +690,7 @@
             r.give.at[n], r.got.at[n], (r.give_send.at[n], r.give_recv.at[n]),
             at(*steps[n]),
         )
+    gather_atoms(r, r.by_atom, r.energy, slots_per)
     spots = hot_columns(r.ghosts[...], count).T.astype(bf16)
     owns = []
     for k in range(3):
@@ -784,8 +799,8 @@
         got=pltpu.VMEM((9, 4, ghost_count), f32),
         move_send=dma((2, 2)),
         move_recv=dma((2, 2)),
-        rows_send=dma((9,)),
-        rows_recv=dma((9,)),
+        rows_send=dma((9, 2)),
+        rows_recv=dma((9, 2)),
         places_send=dma((9,)),
         places_recv=dma((9,)),
         give_send=dma((9,)),

time: 52.8 us -> 51.1 us (0.968)
  Pallas kernels: 50 us -> 48.2 us
    pallas_call x1, Pallas kernels: 50 us -> 48.2 us  [per_device(): pl.pallas_call(functools.partial(whole_kernel, shape, (width, blocks), na...]
where the time goes in v3:
time: 51.1 us; the launch traced here: 50.8 us
  Pallas kernels  48.2 us (94%)
  local copies, waits for them, and re-layouts  1.92 us (4%)
  between operations  0.65 us (1%)
    pallas_call x1, Pallas kernels, per_device(): pl.pallas_call(functools.partial(whole_kernel, shape, (width, blocks), na...  48.2 us
    unnamed x6, local copies, waits for them, and re-layouts  1.92 us

profile of v3, /device:TPU:0, one launch (start us, length us, event | category | flops | bytes accessed | tf_op | source)
XLA Modules:
  0.0 50.8 jit_solution(4917862222682424202)
XLA Ops:
  0.6 48.2 %allegro.1 = (f32[3,1,512]{2,1,0:T(1,128)}, f32[1,512]{1,0:T(1,128)}) custom-call(bf16[512,128]{1,0:T(8,128)(2,1)} %bitcast.13, f32[3,1,512]{2,1,0:T(1,128)} %bitcast.16, s32[2,32]{1,0:T(2,128)} %bitcast.18, s32[2,32]{1,0:T(2,128)} %bitcast.19, s32[1,256]{1,0:T(1,128)} %bitcast.20, s32[16,512]{1,0:T(8,128)} %bitcast.14, bf16[128,128]{1,0:T(8,128)(2,1)} %operands_6_.1, ...), custom_call_target="tpu_custom_call" | custom-call | tf_op jit(solution)/shard_map/allegro/pallas_call | solution.py:811
  48.9 0.0 copy-start
  48.9 0.7 %copy-done = f32[3,1,512]{2,1,0:T(1,128)S(1)} copy-done((f32[3,1,512]{2,1,0:T(1,128)S(1)}, f32[3,1,512]{2,1,0:T(1,128)}, u32[]{:S(2)}) %copy-start) | copy-done | bytes 6168
  49.6 0.0 copy-start.1
  49.6 0.6 %copy.21 = f32[1,1,3,512]{3,1,2,0:T(1,128)} copy(f32[1,1,3,512]{3,1,2,0:T(1,128)S(1)} %bitcast.15) | data formatting | bytes 12288
  50.2 0.1 copy-done.1
  50.2 0.6 %copy.22 = f32[1,1,512]{2,1,0:T(1,128)} copy(f32[1,1,512]{2,1,0:T(1,128)S(1)} %bitcast.17) | data formatting | bytes 4096
Async XLA Ops:
  48.9 0.7 %copy-start = (f32[3,1,512]{2,1,0:T(1,128)S(1)}, f32[3,1,512]{2,1,0:T(1,128)}, u32[]{:S(2)}) copy-start(f32[3,1,512]{2,1,0:T(1,128)} %get-tuple-element.4) | copy-start | bytes 18436
  49.6 0.7 %copy-start.1 = (f32[1,512]{1,0:T(1,128)S(1)}, f32[1,512]{1,0:T(1,128)}, u32[]{:S(2)}) copy-start(f32[1,512]{1,0:T(1,128)} %get-tuple-element.5) | copy-start | bytes 6148

commit v4 on v3

--- a/solution.py
+++ b/solution.py
@@ -146,7 +146,7 @@
             for u in range(2):
                 refs.dense[k, pl.ds(tile + u, 1), :] = far[:, u * lanes : (u + 1) * lanes]
 
-    @pl.loop(0, tiles // 8)
+    @pl.loop(0, tiles // 8, unroll=2)
     def _(group):
         rows = pl.ds(pl.multiple_of(8 * group, 8), 8)
         offsets = [refs.dense[k, rows, :] - refs.dense[3 + k, rows, :] for k in range(3)]
@@ -176,15 +176,13 @@
         blank = jnp.zeros_like(sine)
         left = list(d_top) * 2 + list(d_low) + list(w_top) * 2 + list(w_low) + [blank] * 14
         right = list(w_top) + list(w_low) + list(w_top)
-        other = list(d_top) + list(d_low) + list(d_top)
         values = left + b_top + b_top + b_low + [s_top, s_low] + [blank] * 6
         for n, value in enumerate(values):
             start = pl.multiple_of(group * 512 + n * 8, 8)
             refs.narrow[pl.ds(start, 8), :] = value
-        for n in range(32):
-            start = pl.multiple_of(group * 256 + n * 8, 8)
-            refs.pairs[0, pl.ds(start, 8), :] = right[n] if n < 9 else blank
-            refs.pairs[1, pl.ds(start, 8), :] = other[n - 9] if 9 <= n < 18 else blank
+        for n in range(16):
+            start = pl.multiple_of(group * 128 + n * 8, 8)
+            refs.pairs[pl.ds(start, 8), :] = right[n] if n < 9 else blank
 
 
 def spread_tiles(refs):
@@ -195,11 +193,10 @@
         for member in range(8):
             tile = group * 8 + member
             whole = refs.narrow[pl.ds(group * 512 + member, 64, stride=8), :].astype(bf16)
-            rows = pl.ds(group * 256 + member, 32, stride=8)
+            rows = pl.ds(group * 128 + member, 16, stride=8)
             refs.lead[tile] = whole[:32]
             refs.upright[tile] = whole.T
-            refs.pair[tile, :, :whole.shape[1]] = refs.pairs[0, rows, :].astype(bf16)
-            refs.pair[tile, :, whole.shape[1] :] = refs.pairs[1, rows, :].astype(bf16)
+            refs.pair[tile] = refs.pairs[rows, :].astype(bf16)
 
 
 def gather_tile(refs, table_ref, target, at, tile, count, slots_per, rows):
@@ -218,9 +215,10 @@
     pairs = [refs.pair[tile + u] for u in range(width)]
     stacked = jnp.concatenate(upright, axis=0)
     first = product(stacked, refs.first[...])
-    grams = [product(upright[u][:, :32], pairs[u]) for u in range(width)]
+    grams = [product(upright[u][:, :16], pairs[u]) for u in range(width)]
     yield
     grams = [(x.astype(bf16) * mask) for x in grams]
+    backs = [x.T for x in grams]
     source = jnp.concatenate(
         [
             jnp.broadcast_to(source_ref[pl.ds(a * tiles + tile + u, 1), :], (slots_per, lanes))
@@ -239,7 +237,7 @@
     for layer in range(2):
         around = jnp.concatenate(
             [
-                product(grams[u][:, :lanes], hidden[u * lanes : (u + 1) * lanes]).astype(bf16)
+                product(grams[u], hidden[u * lanes : (u + 1) * lanes]).astype(bf16)
                 for u in range(width)
             ],
             axis=0,
@@ -261,7 +259,7 @@
         turns.append(turn)
         flow = back[:, :lanes] + jnp.concatenate(
             [
-                product(grams[u][:, lanes:], turn[u * lanes : (u + 1) * lanes])
+                product(backs[u], turn[u * lanes : (u + 1) * lanes])
                 for u in range(width)
             ],
             axis=0,
@@ -276,7 +274,7 @@
         cross.append(product_nt(turns[rows], inputs[rows]))
     ends = product_nt(refs.last[...], jnp.concatenate([paired_grad, kept[2]], axis=1))
     yield
-    cross = [x.astype(bf16) * mask[:, :lanes] for x in cross]
+    cross = [x.astype(bf16) * mask for x in cross]
     for u in range(width):
         first_row = pl.multiple_of((tile + u) * 96, 96)
         refs.results[pl.ds(first_row, 32), :] = ends[:, u * lanes : (u + 1) * lanes]
@@ -289,8 +287,8 @@
     count, lanes = source_ref.shape
     tiles = count // 8
     step = width * blocks
-    rows = lax.broadcasted_iota(jnp.int32, (lanes, 2 * lanes), 0) // slots_per
-    cols = (lax.broadcasted_iota(jnp.int32, (lanes, 2 * lanes), 1) & (lanes - 1)) // slots_per
+    rows = lax.broadcasted_iota(jnp.int32, (lanes, lanes), 0) // slots_per
+    cols = lax.broadcasted_iota(jnp.int32, (lanes, lanes), 1) // slots_per
     refs.mask[...] = jnp.where(rows == cols, 1.0, 0.0).astype(bf16)
 
     for tile in range(step):
@@ -346,7 +344,7 @@
     groups = scatter_ref.shape[0] // 3
     scatter_ref[...] = jnp.zeros(scatter_ref.shape, f32)
 
-    @pl.loop(0, tiles // 8)
+    @pl.loop(0, tiles // 8, unroll=2)
     def _(group):
         rows = pl.ds(pl.multiple_of(8 * group, 8), 8)
         offsets = [refs.dense[k, rows, :] for k in range(3)]
@@ -424,14 +422,14 @@
         listed=pltpu.VMEM((tiles, breadth), jnp.int32),
         dense=pltpu.VMEM((6, tiles, breadth), f32),
         narrow=pltpu.VMEM((tiles * 64, breadth), f32),
-        pairs=pltpu.VMEM((2, tiles * 32, breadth), f32),
+        pairs=pltpu.VMEM((tiles * 16, breadth), f32),
         lead=pltpu.VMEM((tiles, 32, breadth), bf16),
         upright=pltpu.VMEM((tiles, breadth, 64), bf16),
-        pair=pltpu.VMEM((tiles, 32, 2 * breadth), bf16),
+        pair=pltpu.VMEM((tiles, 16, breadth), bf16),
         gathered=pltpu.VMEM((width * blocks * breadth, breadth), f32),
         results=pltpu.VMEM((tiles * 96, breadth), f32),
         hot=pltpu.VMEM((tiles // 2, breadth, 2 * breadth), bf16),
-        mask=pltpu.VMEM((breadth, 2 * breadth), bf16),
+        mask=pltpu.VMEM((breadth, breadth), bf16),
         index=pltpu.SMEM((slots_per * count,), jnp.int32),
     )
 

time: 51.1 us -> 49.2 us (0.963)
  Pallas kernels: 48.2 us -> 46.4 us
    pallas_call x1, Pallas kernels: 48.2 us -> 46.4 us  [per_device(): pl.pallas_call(functools.partial(whole_kernel, shape, (width, blocks), na...]
where the time goes in v4:
time: 49.2 us; the launch traced here: 49 us
  Pallas kernels  46.4 us (94%)
  local copies, waits for them, and re-layouts  1.92 us (4%)
  between operations  0.65 us (1%)
    pallas_call x1, Pallas kernels, per_device(): pl.pallas_call(functools.partial(whole_kernel, shape, (width, blocks), na...  46.4 us
    unnamed x6, local copies, waits for them, and re-layouts  1.92 us

profile of v4, /device:TPU:0, one launch (start us, length us, event | category | flops | bytes accessed | tf_op | source)
XLA Modules:
  0.0 49.0 jit_solution(17814524599354559634)
XLA Ops:
  0.6 46.4 %allegro.1 = (f32[3,1,512]{2,1,0:T(1,128)}, f32[1,512]{1,0:T(1,128)}) custom-call(bf16[512,128]{1,0:T(8,128)(2,1)} %bitcast.13, f32[3,1,512]{2,1,0:T(1,128)} %bitcast.16, s32[2,32]{1,0:T(2,128)} %bitcast.18, s32[2,32]{1,0:T(2,128)} %bitcast.19, s32[1,256]{1,0:T(1,128)} %bitcast.20, s32[16,512]{1,0:T(8,128)} %bitcast.14, bf16[128,128]{1,0:T(8,128)(2,1)} %operands_6_.1, ...), custom_call_target="tpu_custom_call" | custom-call | tf_op jit(solution)/shard_map/allegro/pallas_call | solution.py:809
  47.1 0.0 copy-start
  47.1 0.7 %copy-done = f32[3,1,512]{2,1,0:T(1,128)S(1)} copy-done((f32[3,1,512]{2,1,0:T(1,128)S(1)}, f32[3,1,512]{2,1,0:T(1,128)}, u32[]{:S(2)}) %copy-start) | copy-done | bytes 6168
  47.7 0.0 copy-start.1
  47.7 0.6 %copy.21 = f32[1,1,3,512]{3,1,2,0:T(1,128)} copy(f32[1,1,3,512]{3,1,2,0:T(1,128)S(1)} %bitcast.15) | data formatting | bytes 12288
  48.3 0.1 copy-done.1
  48.4 0.6 %copy.22 = f32[1,1,512]{2,1,0:T(1,128)} copy(f32[1,1,512]{2,1,0:T(1,128)S(1)} %bitcast.17) | data formatting | bytes 4096
Async XLA Ops:
  47.1 0.7 %copy-start = (f32[3,1,512]{2,1,0:T(1,128)S(1)}, f32[3,1,512]{2,1,0:T(1,128)}, u32[]{:S(2)}) copy-start(f32[3,1,512]{2,1,0:T(1,128)} %get-tuple-element.4) | copy-start | bytes 18436
  47.7 0.7 %copy-start.1 = (f32[1,512]{1,0:T(1,128)S(1)}, f32[1,512]{1,0:T(1,128)}, u32[]{:S(2)}) copy-start(f32[1,512]{1,0:T(1,128)} %get-tuple-element.5) | copy-start | bytes 6148

commit v5 on v4

--- a/solution.py
+++ b/solution.py
@@ -506,15 +506,10 @@
             (r.ghosts_far, r.ghosts),
             (r.source_weight_far, r.source_weight),
             (r.target_weight_far, r.target_weight),
+            (r.coords_far, r.coords),
+            (r.neighbours_far, r.neighbours),
         ],
         r.fetch_sem,
-    )
-    lists = fetch_all(
-        [
-            (r.neighbours.at[slot], r.index.at[pl.ds(slot * count, count)])
-            for slot in range(slots_per)
-        ],
-        r.index_sem,
     )
     later = fetch_all(
         [
@@ -530,6 +525,15 @@
         r.later_sem,
     )
 
+    for fetch in fetches:
+        fetch.wait()
+    lists = fetch_all(
+        [
+            (r.neighbours.at[slot], r.index.at[pl.ds(slot * count, count)])
+            for slot in range(slots_per)
+        ],
+        r.index_sem,
+    )
     holding = r.holding
     blank = jnp.zeros((5, count), f32)
     pieces = []
@@ -537,8 +541,6 @@
         pieces += [piece, blank]
     pieces.append(jnp.zeros((breadth - 24, count), f32))
     holding[:, breadth:] = jnp.concatenate(pieces, axis=0).T.astype(bf16)
-    for fetch in fetches:
-        fetch.wait()
     holding[:, :breadth] = r.features[...]
     moves = [
         jnp.concatenate([n[0:1, :], n[1:2, :]], axis=1) for n in (r.slots_x, r.slots_y)
@@ -746,11 +748,11 @@
     square = pltpu.VMEM((breadth, breadth), bf16)
     inputs = dict(
         features_far=features,
-        coords=coords,
+        coords_far=coords,
         slots_x_far=migrate_x_slots[0, 0],
         slots_y_far=migrate_y_slots[0, 0],
         ghosts_far=ghosts,
-        neighbours=neighbours,
+        neighbours_far=neighbours,
         source_weight_far=source_weight,
         target_weight_far=target_weight,
         radial_far=radial_weight,
@@ -777,7 +779,9 @@
         environ_second=square,
         mixing_second=square,
         coupler_second=square,
-        fetch_sem=dma((6,)),
+        coords=pltpu.VMEM((3, 1, count), f32),
+        neighbours=pltpu.VMEM((slots_per, count), jnp.int32),
+        fetch_sem=dma((8,)),
         index_sem=dma((slots_per,)),
         later_sem=dma((8,)),
         table=pltpu.VMEM((total_rows, breadth), f32),
@@ -812,7 +816,7 @@
             jax.ShapeDtypeStruct((3, 1, count), f32),
             jax.ShapeDtypeStruct((1, count), f32),
         ),
-        in_specs=[vmem if n in ("coords", "neighbours") else hbm for n in inputs],
+        in_specs=[hbm] * len(inputs),
         out_specs=(vmem,) * 2,
         scratch_shapes=list(scratch.values()),
         compiler_params=pltpu.CompilerParams(

time: 49.2 us -> 48.7 us (0.990)
  Pallas kernels: 46.4 us -> 45.9 us
    pallas_call x1, Pallas kernels: 46.4 us -> 45.9 us  [per_device(): pl.pallas_call(functools.partial(whole_kernel, shape, (width, blocks), na...]
where the time goes in v5:
time: 48.7 us; the launch traced here: 48.5 us
  Pallas kernels  45.9 us (94%)
  local copies, waits for them, and re-layouts  1.92 us (4%)
  between operations  0.65 us (1%)
    pallas_call x1, Pallas kernels, per_device(): pl.pallas_call(functools.partial(whole_kernel, shape, (width, blocks), na...  45.9 us
    unnamed x6, local copies, waits for them, and re-layouts  1.92 us

profile of v5, /device:TPU:0, one launch (start us, length us, event | category | flops | bytes accessed | tf_op | source)
XLA Modules:
  0.0 48.5 jit_solution(11660337353585376122)
XLA Ops:
  0.6 45.9 %allegro.1 = (f32[3,1,512]{2,1,0:T(1,128)}, f32[1,512]{1,0:T(1,128)}) custom-call(bf16[512,128]{1,0:T(8,128)(2,1)} %bitcast.13, f32[3,1,512]{2,1,0:T(1,128)} %bitcast.16, s32[2,32]{1,0:T(2,128)} %bitcast.18, s32[2,32]{1,0:T(2,128)} %bitcast.19, s32[1,256]{1,0:T(1,128)} %bitcast.20, s32[16,512]{1,0:T(8,128)} %bitcast.14, bf16[128,128]{1,0:T(8,128)(2,1)} %operands_6_.1, ...), custom_call_target="tpu_custom_call" | custom-call | tf_op jit(solution)/shard_map/allegro/pallas_call | solution.py:813
  46.5 0.0 copy-start
  46.5 0.7 %copy-done = f32[3,1,512]{2,1,0:T(1,128)S(1)} copy-done((f32[3,1,512]{2,1,0:T(1,128)S(1)}, f32[3,1,512]{2,1,0:T(1,128)}, u32[]{:S(2)}) %copy-start) | copy-done | bytes 6168
  47.2 0.0 copy-start.1
  47.2 0.6 %copy.21 = f32[1,1,3,512]{3,1,2,0:T(1,128)} copy(f32[1,1,3,512]{3,1,2,0:T(1,128)S(1)} %bitcast.15) | data formatting | bytes 12288
  47.8 0.1 copy-done.1
  47.9 0.6 %copy.22 = f32[1,1,512]{2,1,0:T(1,128)} copy(f32[1,1,512]{2,1,0:T(1,128)S(1)} %bitcast.17) | data formatting | bytes 4096
Async XLA Ops:
  46.5 0.7 %copy-start = (f32[3,1,512]{2,1,0:T(1,128)S(1)}, f32[3,1,512]{2,1,0:T(1,128)}, u32[]{:S(2)}) copy-start(f32[3,1,512]{2,1,0:T(1,128)} %get-tuple-element.4) | copy-start | bytes 18436
  47.2 0.7 %copy-start.1 = (f32[1,512]{1,0:T(1,128)S(1)}, f32[1,512]{1,0:T(1,128)}, u32[]{:S(2)}) copy-start(f32[1,512]{1,0:T(1,128)} %get-tuple-element.5) | copy-start | bytes 6148
